TPU v7x, 32 devices: a whole 2x2x4 slice. The times are simulated.
32 devices in a mesh: dom: 16 (over z, x, core), head: 2 (over y).
Axes of the slice: x: 2, y: 2, z: 4, core: 2. Of those that a mesh axis runs over, the one named last changes fastest.
Arguments:
- node_feats: bfloat16 [32768, 512], P(('dom', 'head')), may hold values from -16 to 16
- w_qkv: bfloat16 [512, 1536], replicated, may hold values from -1 to 1
- w_out: bfloat16 [512, 512], replicated, may hold values from -2 to 2
- neighbours: int32 [256, 4], P('dom'), may hold values from 0 to 15
- tiles: int32 [256, 4, 128, 128], P('dom'), may hold values 0 or 1
- partner: int32 [256], P('dom'), may hold values from 0 to 255, as said below
- layer_cot: bfloat16 [32768, 512], P(('dom', 'head')), may hold values from -6 to 6
Outputs:
- layer_out: bfloat16 [32768, 512], P(('dom', 'head'))
- feat_grad: bfloat16 [32768, 512], P(('dom', 'head'))
- dw_qkv: float32 [512, 1536], P('dom', 'head')
- dw_out: float32 [512, 512], P('head', 'dom')
Inputs may be any that keep to these rules, and one draw needn't show every extreme that they name: partner is a perfect matching of the 256 node blocks: partner[partner[b]] = b, and the partner of a block lies in another part (part = block // 16). For every two parts, at most 2 blocks of one are matched to blocks of the other, and some two parts have exactly 2 such pairs.
All inputs are finite; a program needn't handle non-finite values. No bound on the sum of `tiles` on one device may be relied on, other than what follows from the above.
Results may differ from a plain program's by a relative error of at most 0.019.
The roundings to bfloat16 on the way count: a program that leaves them out, or rounds other values in their place, can miss the bound.
Values may be sent and summed in bfloat16 or wider, within the bound.
A program may use at most 192 MiB of HBM per device.

v0:
```python
import jax
import jax.numpy as jnp
from jax import lax
from jax.sharding import PartitionSpec as P

H = 8
NBR = 4
GB = 4


def body(node_feats, w_qkv, w_out, neighbours, tiles, partner, layer_cot):
    rows, width = node_feats.shape
    groups = lax.axis_size("head")
    parts = lax.axis_size("dom")
    blocks = partner.shape[0]
    block_size = tiles.shape[2]
    head_dim = width // H
    group_heads = H // groups
    span = group_heads * head_dim
    slots = (blocks + parts - 2) // (parts - 1)
    scale = head_dim ** (-0.5)
    part_rows = blocks * block_size
    qkv_node = jnp.dot(node_feats, w_qkv, preferred_element_type=jnp.float32).astype(jnp.bfloat16)
    qkv_part = lax.all_to_all(
        qkv_node.reshape(rows, groups, 3 * span), "head", split_axis=1, concat_axis=0, tiled=True
    )
    qkv_part = qkv_part.reshape(part_rows, 3 * span)
    query_all = qkv_part[:, :span].reshape(blocks, block_size, span)
    kv_all = qkv_part[:, span:].reshape(blocks, block_size, 2 * span)
    target = partner // blocks
    block_iota = jnp.arange(blocks, dtype=jnp.int32)
    same_target = target[:, None] == target[None, :]
    earlier = block_iota[None, :] < block_iota[:, None]
    lower = partner[None, :] < partner[:, None]
    send_slot = target * slots + jnp.sum((same_target & earlier).astype(jnp.int32), axis=1)
    recv_slot = target * slots + jnp.sum((same_target & lower).astype(jnp.int32), axis=1)
    outgoing = (
        jnp.zeros((parts * slots, block_size, 2 * span), jnp.bfloat16).at[send_slot].set(kv_all)
    )
    incoming = lax.all_to_all(outgoing, "dom", split_axis=0, concat_axis=0, tiled=True)
    kv_partner = incoming[recv_slot]

    def key_sets(start):
        ids = lax.dynamic_slice_in_dim(neighbours, start, GB, 0)
        near_kv = kv_all[ids].reshape(GB, NBR * block_size, 2 * span)
        far_kv = lax.dynamic_slice_in_dim(kv_partner, start, GB, 0)
        joined = jnp.concatenate([near_kv, far_kv], axis=1)
        key_four = joined[..., :span].reshape(GB, (NBR + 1) * block_size, group_heads, head_dim)
        value_four = joined[..., span:].reshape(GB, (NBR + 1) * block_size, group_heads, head_dim)
        tile_block = lax.dynamic_slice_in_dim(tiles, start, GB, 0)
        visible = jnp.concatenate(
            [
                tile_block.transpose(0, 2, 1, 3).reshape(GB, block_size, NBR * block_size) != 0,
                jnp.ones((GB, block_size, block_size), dtype=jnp.bool_),
            ],
            axis=2,
        )
        query_four = lax.dynamic_slice_in_dim(query_all, start, GB, 0).reshape(
            GB, block_size, group_heads, head_dim
        )
        scores = (
            jnp.einsum("bqhd,bkhd->bhqk", query_four, key_four, preferred_element_type=jnp.float32)
            * scale
        )
        scores = jnp.where(visible[:, None], scores, -1e30)
        return (ids, query_four, key_four, value_four, scores)

    def forward_step(start):
        ids, query_four, key_four, value_four, scores = key_sets(start)
        peak = jnp.max(scores, axis=-1)
        total = jnp.sum(jnp.exp(scores - peak[..., None]), axis=-1)
        probs_low = (jnp.exp(scores - peak[..., None]) / total[..., None]).astype(jnp.bfloat16)
        attended = jnp.einsum(
            "bhqk,bkhd->bqhd", probs_low, value_four, preferred_element_type=jnp.float32
        )
        return (attended.astype(jnp.bfloat16).reshape(GB, block_size, span), peak, total)

    starts = jnp.arange(0, blocks, GB, dtype=jnp.int32)
    attended_all, peak_all, total_all = lax.map(forward_step, starts)
    attended_all = attended_all.reshape(blocks, block_size, span)
    peak_all = peak_all.reshape(blocks, group_heads, block_size)
    total_all = total_all.reshape(blocks, group_heads, block_size)
    attended_part = attended_all.reshape(part_rows, span)
    attended_node = lax.all_to_all(attended_part, "head", split_axis=0, concat_axis=1, tiled=True)
    layer_out = jnp.dot(attended_node, w_out, preferred_element_type=jnp.float32).astype(
        jnp.bfloat16
    )
    cot_node = jnp.dot(layer_cot, w_out.T, preferred_element_type=jnp.float32).astype(jnp.bfloat16)
    cot_part = lax.all_to_all(cot_node, "head", split_axis=1, concat_axis=0, tiled=True)
    cot_all = cot_part.reshape(blocks, block_size, span)
    delta_all = jnp.sum(
        (cot_all.astype(jnp.float32) * attended_all.astype(jnp.float32)).reshape(
            blocks, block_size, group_heads, head_dim
        ),
        axis=-1,
    ).transpose(0, 2, 1)
    reach = (NBR + 1) * block_size

    def backward_step(accum, start):
        ids, query_four, key_four, value_four, scores = key_sets(start)
        peak = lax.dynamic_slice_in_dim(peak_all, start, GB, 0)
        total = lax.dynamic_slice_in_dim(total_all, start, GB, 0)
        delta = lax.dynamic_slice_in_dim(delta_all, start, GB, 0)
        probs = jnp.exp(scores - peak[..., None]) / total[..., None]
        probs_low = probs.astype(jnp.bfloat16)
        grad_four = lax.dynamic_slice_in_dim(cot_all, start, GB, 0).reshape(
            GB, block_size, group_heads, head_dim
        )
        grad_probs = jnp.einsum(
            "bqhd,bkhd->bhqk", grad_four, value_four, preferred_element_type=jnp.float32
        )
        grad_scores = (probs * (grad_probs - delta[..., None]) * scale).astype(jnp.bfloat16)
        grad_query = jnp.einsum(
            "bhqk,bkhd->bqhd", grad_scores, key_four, preferred_element_type=jnp.float32
        )
        grad_keys = jnp.einsum(
            "bhqk,bqhd->bkhd", grad_scores, query_four, preferred_element_type=jnp.float32
        )
        grad_values = jnp.einsum(
            "bhqk,bqhd->bkhd", probs_low, grad_four, preferred_element_type=jnp.float32
        )
        joined_grad = jnp.concatenate(
            [grad_keys.reshape(GB, reach, span), grad_values.reshape(GB, reach, span)], axis=-1
        )
        near_grad = joined_grad[:, : NBR * block_size].reshape(GB * NBR, block_size, 2 * span)
        one_hot = (ids.reshape(-1)[:, None] == block_iota[None, :]).astype(jnp.float32)
        accum = accum + jnp.einsum(
            "jb,jrc->brc", one_hot, near_grad, precision=lax.Precision.HIGHEST
        )
        query_flat = grad_query.reshape(GB, block_size, span)
        outputs = (query_flat, joined_grad[:, NBR * block_size :].astype(jnp.bfloat16))
        return (accum, outputs)

    zero_accum = jnp.zeros((blocks, block_size, 2 * span), jnp.float32)
    accum, outputs = lax.scan(backward_step, zero_accum, starts)
    grad_query_all = outputs[0].reshape(blocks, block_size, span)
    far_all = outputs[1].reshape(blocks, block_size, 2 * span)
    buffer = (
        jnp.zeros((parts * slots, block_size, 2 * span), jnp.bfloat16).at[recv_slot].set(far_all)
    )
    returned = lax.all_to_all(buffer, "dom", split_axis=0, concat_axis=0, tiled=True)
    accum = accum + returned[send_slot].astype(jnp.float32)
    dqkv_part = (
        jnp.concatenate([grad_query_all, accum], axis=-1)
        .reshape(part_rows, 3 * span)
        .astype(jnp.bfloat16)
    )
    dqkv_node = lax.all_to_all(dqkv_part, "head", split_axis=0, concat_axis=1, tiled=True)
    feat_grad = jnp.dot(dqkv_node, w_qkv.T, preferred_element_type=jnp.float32).astype(jnp.bfloat16)
    full_qkv = jnp.einsum("rd,rc->dc", node_feats, dqkv_node, preferred_element_type=jnp.float32)
    full_out = jnp.einsum("rd,rc->dc", attended_node, layer_cot, preferred_element_type=jnp.float32)
    grad_qkv, grad_out = (
        lax.psum_scatter(
            full_qkv.astype(jnp.bfloat16), "head", scatter_dimension=1, tiled=True
        ).astype(jnp.float32),
        lax.psum_scatter(
            full_out.astype(jnp.bfloat16), "head", scatter_dimension=0, tiled=True
        ).astype(jnp.float32),
    )
    dw_qkv, dw_out = (
        lax.psum_scatter(grad_qkv, "dom", scatter_dimension=0, tiled=True),
        lax.psum_scatter(grad_out, "dom", scatter_dimension=1, tiled=True),
    )
    return (layer_out, feat_grad, dw_qkv, dw_out)


def solution(mesh):
    placed = (
        P(("dom", "head"), None),
        P(),
        P(),
        P("dom", None),
        P("dom", None, None, None),
        P("dom"),
        P(("dom", "head"), None),
    )
    return jax.shard_map(
        body,
        mesh=mesh,
        in_specs=placed,
        out_specs=(
            P(("dom", "head"), None),
            P(("dom", "head"), None),
            P("dom", "head"),
            P("head", "dom"),
        ),
        check_vma=False,
    )
```

profile of v0, /device:TPU:0, one launch (start us, length us, event | category | flops | bytes accessed | tf_op | source)
XLA Modules:
  0.0 848.9 jit_solution(8154592767609231499)
XLA Ops:
  13.4 5.4 all-to-all-start
  22.1 34.4 %all-to-all-done = bf16[1024,2,768]{2,0,1:T(8,128)(2,1)} async-done(((bf16[1024,2,768]{2,0,1:T(8,128)(2,1)}), bf16[1024,2,768]{2,0,1:T(8,128)(2,1)}, u32[]{:S(2)}, u32[]{:S(2)}) %all-to-all-start) | async-done | bytes 3145760 | tf_op jit(solution)/shard_map/all_to_all | solution.py:24
  65.9 6.0 scatter_fusion
  73.4 5.9 all-to-all-start.1
  79.4 7.1 copy.78
  88.0 4.2 copy.83
  92.2 3.9 reshape.131
  98.7 58.1 %all-to-all-done.1 = bf16[32,128,512]{2,1,0:T(8,128)(2,1)} async-done(((bf16[32,128,512]{2,1,0:T(8,128)(2,1)}), bf16[32,128,512]{2,1,0:T(8,128)(2,1)}, u32[]{:S(2)}, u32[]{:S(2)}) %all-to-all-start.1) | async-done | bytes 4194336 | tf_op jit(solution)/shard_map/all_to_all | solution.py:40
  156.8 4.3 gather_fusion.2
  161.1 3.9 copy.77
  165.0 91.3 %while.29 = (s32[]{:T(128)}, bf16[4,4,128,256]{2,3,1,0:T(8,128)(2,1)}, f32[4,4,4,128]{3,2,1,0:T(4,128)S(1)}, f32[4,4,4,128]{3,2,1,0:T(4,128)S(1)}, s32[4]{0:T(12...) while((s32[]{:T(128)}, ...), condition=%wide.region_6.7_spmd, body=%wide.region_3.6_spmd.sunk | while | flops 356906048 | bytes 43332708 | solution.py:79
  171.4 4.2 copy.123
  194.2 4.2 copy.123
  217.1 4.2 copy.123
  239.9 4.2 copy.123
  258.7 239.8 %while.30 = (s32[]{:T(128)}, f32[16,128,512]{2,0,1:T(8,128)}, bf16[4,4,128,256]{3,2,1,0:T(8,128)(2,1)}, bf16[4,4,128,512]{3,2,1,0:T(8,128)(2,1)}, s32[4]{0:T(128...) while((s32[]{:T(128)}, f32[16,128,512]{2,0,1:T(8,128)}, ...), condition=%wide.region_9.10_spmd.clone, body=%wide.region_8.9_spmd.clone.sunk | while | flops 1061684544 | bytes 134445024 | solution.py:135
  261.6 3.6 gather_fusion.1
  265.2 4.1 copy.125
  283.9 3.8 multiply_convert_fusion.2
  293.6 4.6 fusion.99
  307.2 8.7 %select_add_fusion.2 = f32[16,128,512]{2,0,1:T(8,128)} fusion(f32[16,128,512]{2,0,1:T(8,128)} %get-tuple-element.597, f32[16,128,512]{2,1,0:T(8,128)} %bitcast.164, pred[]{:T(512)S(6)} %compare.7, s32[16]{0:T(128)S(1)} %eq.58), kind=kOutput, calls=%fused_computation.36.clone.1 | convolution fusion | flops 203424000 | bytes 12582977 | tf_op jit(solution)/shard_map/while/body/eval_jaxpr/jb,jrc->brc/dot_general | solution.py:127
  320.6 3.6 gather_fusion.1
  324.2 4.1 copy.125
  342.9 3.8 multiply_convert_fusion.2
  352.5 4.6 fusion.99
  366.1 10.0 %select_add_fusion.2 = f32[16,128,512]{2,0,1:T(8,128)} fusion(f32[16,128,512]{2,0,1:T(8,128)} %get-tuple-element.597, f32[16,128,512]{2,1,0:T(8,128)} %bitcast.164, pred[]{:T(512)S(6)} %compare.7, s32[16]{0:T(128)S(1)} %eq.58), kind=kOutput, calls=%fused_computation.36.clone.1 | convolution fusion | flops 203424000 | bytes 12582977 | tf_op jit(solution)/shard_map/while/body/eval_jaxpr/jb,jrc->brc/dot_general | solution.py:127
  384.4 4.1 copy.125
  403.1 3.8 multiply_convert_fusion.2
  412.7 4.6 fusion.99
  426.3 10.0 %select_add_fusion.2 = f32[16,128,512]{2,0,1:T(8,128)} fusion(f32[16,128,512]{2,0,1:T(8,128)} %get-tuple-element.597, f32[16,128,512]{2,1,0:T(8,128)} %bitcast.164, pred[]{:T(512)S(6)} %compare.7, s32[16]{0:T(128)S(1)} %eq.58), kind=kOutput, calls=%fused_computation.36.clone.1 | convolution fusion | flops 203424000 | bytes 12582977 | tf_op jit(solution)/shard_map/while/body/eval_jaxpr/jb,jrc->brc/dot_general | solution.py:127
  440.9 3.6 gather_fusion.1
  444.5 4.1 copy.125
  463.2 3.8 multiply_convert_fusion.2
  472.9 4.6 fusion.99
  486.5 10.0 %select_add_fusion.2 = f32[16,128,512]{2,0,1:T(8,128)} fusion(f32[16,128,512]{2,0,1:T(8,128)} %get-tuple-element.597, f32[16,128,512]{2,1,0:T(8,128)} %bitcast.164, pred[]{:T(512)S(6)} %compare.7, s32[16]{0:T(128)S(1)} %eq.58), kind=kOutput, calls=%fused_computation.36.clone.1 | convolution fusion | flops 203424000 | bytes 12582977 | tf_op jit(solution)/shard_map/while/body/eval_jaxpr/jb,jrc->brc/dot_general | solution.py:127
  501.0 6.0 scatter_fusion.1
  507.1 19.8 %all-to-all-start.4 = ((bf16[32,128,512]{2,1,0:T(8,128)(2,1)}), bf16[32,128,512]{2,1,0:T(8,128)(2,1)}, u32[]{:S(2)}, u32[]{:S(2)}) async-start(bf16[32,128,512]{2,1,0:T(8,128)(2,1)} %scatter_fusion.1), calls=%async_computation.4 | async-start | bytes 8388608 | tf_op jit(solution)/shard_map/all_to_all | solution.py:141
  528.2 76.2 %all-to-all-done.4 = bf16[32,128,512]{2,1,0:T(8,128)(2,1)} async-done(((bf16[32,128,512]{2,1,0:T(8,128)(2,1)}), bf16[32,128,512]{2,1,0:T(8,128)(2,1)}, u32[]{:S(2)}, u32[]{:S(2)}) %all-to-all-start.4) | async-done | bytes 4194336 | tf_op jit(solution)/shard_map/all_to_all | solution.py:141
  608.0 4.2 gather_fusion.3
  612.2 5.3 fusion.25
  619.4 3.6 all-to-all-done.2
  623.0 5.2 all-to-all-start.5
  632.7 37.8 %all-to-all-done.5 = bf16[2,1024,768]{2,1,0:T(8,128)(2,1)} async-done(((bf16[2,1024,768]{2,1,0:T(8,128)(2,1)}), bf16[2,1024,768]{2,1,0:T(8,128)(2,1)}, u32[]{:S(2)}, u32[]{:S(2)}) %all-to-all-start.5) | async-done | bytes 3145760 | tf_op jit(solution)/shard_map/all_to_all | solution.py:148
  670.5 4.7 copy.93
  675.3 4.9 fusion.26
  682.3 37.0 %reduce-scatter.9.cloned.1.call-done = bf16[512,768]{0,1:T(8,128)(2,1)} async-done(((bf16[512,1536]{0,1:T(8,128)(2,1)}), bf16[512,768]{0,1:T(8,128)(2,1)}) %reduce-scatter.9.cloned.1.call-update) | async-done | bytes 786448 | tf_op jit(solution)/shard_map/reduce_scatter | solution.py:153
  727.0 52.6 %reduce-scatter.15.cloned.1.call-done = f32[32,256]{1,0:T(8,128)} async-done(((f32[512,256]{1,0:T(8,128)}), f32[32,256]{1,0:T(8,128)}) %reduce-scatter.15.cloned.1.call-update) | async-done | bytes 32784
  779.7 62.7 %reduce-scatter.13.cloned.1.call-done = f32[32,768]{1,0:T(8,128)} async-done(((f32[512,768]{1,0:T(8,128)}), f32[32,768]{1,0:T(8,128)}) %reduce-scatter.13.cloned.1.call-update) | async-done | bytes 98320
  (282 shorter events, 248.1 us)
Async XLA Ops:
  7.2 1.4 copy-start
  13.4 5.4 copy-start.19
  13.4 43.1 %all-to-all-start = ((bf16[1024,2,768]{2,0,1:T(8,128)(2,1)}), bf16[1024,2,768]{2,0,1:T(8,128)(2,1)}, u32[]{:S(2)}, u32[]{:S(2)}) async-start(bf16[1024,2,768]{2,0,1:T(8,128)(2,1)} %bitcast.182), calls=%async_computation | async-start | bytes 6291456 | tf_op jit(solution)/shard_map/all_to_all | solution.py:24
  20.8 39.3 %copy-start.16 = (s32[16]{0:T(128)S(1)}, s32[16]{0:T(128)}, u32[]{:S(2)}) copy-start(s32[16]{0:T(128)} %param.16) | copy-start | bytes 196
  56.5 16.9 %all-to-all-start.3 = ((bf16[1024,2,256]{2,0,1:T(8,128)(2,1)}), bf16[1024,2,256]{2,0,1:T(8,128)(2,1)S(1)}, u32[]{:S(2)}, u32[]{:S(2)}) async-start(bf16[1024,2,256]{2,0,1:T(8,128)(2,1)} %copy.82), calls=%async_computation.3 | async-start | bytes 2097152 | tf_op jit(solution)/shard_map/all_to_all | solution.py:89
  60.3 5.6 copy-start.12
  60.3 26.2 %copy-start.14 = (s32[16]{0:T(128)}, s32[16]{0:T(128)S(1)}, u32[]{:S(2)}) copy-start(s32[16]{0:T(128)S(1)} %get-tuple-element.364) | copy-start | bytes 196
  73.4 13.1 %copy-start.6 = (bf16[1024,2,256]{2,0,1:T(8,128)(2,1)}, bf16[1024,2,256]{2,0,1:T(8,128)(2,1)S(1)}, u32[]{:S(2)}) copy-start(bf16[1024,2,256]{2,0,1:T(8,128)(2,1)S(1)} %all-to-all-done.3) | copy-start | bytes 3145732
  73.4 83.5 %all-to-all-start.1 = ((bf16[32,128,512]{2,1,0:T(8,128)(2,1)}), bf16[32,128,512]{2,1,0:T(8,128)(2,1)}, u32[]{:S(2)}, u32[]{:S(2)}) async-start(bf16[32,128,512]{2,1,0:T(8,128)(2,1)} %scatter_fusion), calls=%async_computation.1 | async-start | bytes 8388608 | tf_op jit(solution)/shard_map/all_to_all | solution.py:40
  79.3 7.1 copy-start.17
  183.5 1.5 copy-start.5
  206.3 1.5 copy-start.5
  229.1 1.5 copy-start.5
  252.0 1.5 copy-start.5
  256.3 2.2 copy-start.7
  287.8 2.5 copy-start.1
  301.5 2.2 copy-start.3
  301.5 3.0 copy-start.4
  307.2 8.7 %copy-start.2 = (bf16[4,4,128,640]{3,2,1,0:T(8,128)(2,1)S(1)}, bf16[4,4,128,640]{3,2,1,0:T(8,128)(2,1)}, u32[]{:S(2)}) copy-start(bf16[4,4,128,640]{3,2,1,0:T(8,128)(2,1)} %copy-done.1) | copy-start | bytes 7864324 | tf_op jit(solution)/shard_map/while
  346.7 2.5 copy-start.1
  360.4 2.2 copy-start.3
  360.4 3.0 copy-start.4
  366.1 10.0 %copy-start.2 = (bf16[4,4,128,640]{3,2,1,0:T(8,128)(2,1)S(1)}, bf16[4,4,128,640]{3,2,1,0:T(8,128)(2,1)}, u32[]{:S(2)}) copy-start(bf16[4,4,128,640]{3,2,1,0:T(8,128)(2,1)} %copy-done.1) | copy-start | bytes 7864324 | tf_op jit(solution)/shard_map/while
  406.9 2.5 copy-start.1
  420.6 2.2 copy-start.3
  420.6 3.0 copy-start.4
  426.3 10.0 %copy-start.2 = (bf16[4,4,128,640]{3,2,1,0:T(8,128)(2,1)S(1)}, bf16[4,4,128,640]{3,2,1,0:T(8,128)(2,1)}, u32[]{:S(2)}) copy-start(bf16[4,4,128,640]{3,2,1,0:T(8,128)(2,1)} %copy-done.1) | copy-start | bytes 7864324 | tf_op jit(solution)/shard_map/while
  467.1 2.5 copy-start.1
  480.8 2.2 copy-start.3
  480.8 3.0 copy-start.4
  486.5 10.0 %copy-start.2 = (bf16[4,4,128,640]{3,2,1,0:T(8,128)(2,1)S(1)}, bf16[4,4,128,640]{3,2,1,0:T(8,128)(2,1)}, u32[]{:S(2)}) copy-start(bf16[4,4,128,640]{3,2,1,0:T(8,128)(2,1)} %copy-done.1) | copy-start | bytes 7864324 | tf_op jit(solution)/shard_map/while
  498.5 2.5 copy-start.15
  507.1 19.8 %copy-start.13 = (s32[16]{0:T(128)S(1)}, s32[16]{0:T(128)}, u32[]{:S(2)}) copy-start(s32[16]{0:T(128)} %copy-done.12) | copy-start | bytes 196
  507.1 19.8 %copy-start.8 = (bf16[4,4,128,256]{2,3,1,0:T(8,128)(2,1)S(1)}, bf16[4,4,128,256]{2,3,1,0:T(8,128)(2,1)}, u32[]{:S(2)}) copy-start(bf16[4,4,128,256]{2,3,1,0:T(8,128)(2,1)} %get-tuple-element.137) | copy-start | bytes 3145732
  507.1 97.3 %all-to-all-start.4 = ((bf16[32,128,512]{2,1,0:T(8,128)(2,1)}), bf16[32,128,512]{2,1,0:T(8,128)(2,1)}, u32[]{:S(2)}, u32[]{:S(2)}) async-start(bf16[32,128,512]{2,1,0:T(8,128)(2,1)} %scatter_fusion.1), calls=%async_computation.4 | async-start | bytes 8388608 | tf_op jit(solution)/shard_map/all_to_all | solution.py:141
  604.4 18.6 %all-to-all-start.2 = ((bf16[2,1024,256]{2,1,0:T(8,128)(2,1)}), bf16[2,1024,256]{2,1,0:T(8,128)(2,1)S(1)}, u32[]{:S(2)}, u32[]{:S(2)}) async-start(bf16[2,1024,256]{2,1,0:T(8,128)(2,1)} %bitcast.188), calls=%async_computation.2 | async-start | bytes 2097152 | tf_op jit(solution)/shard_map/all_to_all | solution.py:84
  612.2 5.3 copy-start.11
  623.0 47.5 %all-to-all-start.5 = ((bf16[2,1024,768]{2,1,0:T(8,128)(2,1)}), bf16[2,1024,768]{2,1,0:T(8,128)(2,1)}, u32[]{:S(2)}, u32[]{:S(2)}) async-start(bf16[2,1024,768]{2,1,0:T(8,128)(2,1)} %pad_maximum_fusion.3), calls=%async_computation.5 | async-start | bytes 6291456 | tf_op jit(solution)/shard_map/all_to_all | solution.py:148
  628.2 52.1 %reduce-scatter.11.cloned.1.call-start = ((), (), s32[]{:S(2)}) async-start(), calls=%async_computation.11 | async-start | bytes 786432 | tf_op jit(solution)/shard_map/reduce_scatter | solution.py:156
  632.6 86.7 %reduce-scatter.9.cloned.1.call-start = ((), (), s32[]{:S(2)}) async-start(), calls=%async_computation.10 | async-start | bytes 2359296 | tf_op jit(solution)/shard_map/reduce_scatter | solution.py:153
  670.5 4.7 copy-start.18
  680.1 41.8 %copy-start.10 = (bf16[1024,2,256]{0,2,1:T(8,128)(2,1)S(1)}, bf16[1024,2,256]{0,2,1:T(8,128)(2,1)}, u32[]{:S(2)}) copy-start(bf16[1024,2,256]{0,2,1:T(8,128)(2,1)} %copy.81) | copy-start | bytes 3145732
  680.2 41.8 %copy-start.20 = (bf16[512,512]{1,0:T(8,128)(2,1)S(1)}, bf16[512,512]{1,0:T(8,128)(2,1)}, u32[]{:S(2)}) copy-start(bf16[512,512]{1,0:T(8,128)(2,1)} %param.13) | copy-start | bytes 1572868
  680.2 99.5 %reduce-scatter.15.cloned.1.call-start = ((), (), s32[]{:S(2)}) async-start(), calls=%async_computation.13 | async-start | bytes 557056
  682.3 160.1 %reduce-scatter.13.cloned.1.call-start = ((), (), s32[]{:S(2)}) async-start(), calls=%async_computation.12 | async-start | bytes 1671168
  722.0 2.3 copy-start.9
Sparse Core Ops, SparseCore 0:
  632.7 35.1 reduce-scatter.10
  680.3 39.0 reduce-scatter.8
  723.5 56.1 reduce-scatter.14
  783.8 58.5 reduce-scatter.12
where the time goes:
time: 853 us; the launch traced here: 849 us
  waiting for transfers between devices  364 us (43%)
  local copies, waits for them, and re-layouts  210 us (25%)
  matrix products  131 us (15%)
  other arithmetic  69.5 us (8%)
  starting transfers between devices  43.6 us (5%)
  loops' own time  17 us (2%)
  between operations  14.1 us (2%)
    unnamed x6, waiting for transfers between devices  115 us
    all_to_all x1, waiting for transfers between devices, body(): lax.all_to_all(buffer, 'dom', split_axis=0, concat_axis=0, tiled=True)  76.2 us
    all_to_all x1, waiting for transfers between devices, body(): lax.all_to_all(outgoing, 'dom', split_axis=0, concat_axis=0, tiled=True)  58.1 us
    dot_general x4, matrix products, backward_step(): jnp.einsum('jb,jrc->brc', one_hot, near_grad, precision=lax.Precision.HIG...  38.7 us
    all_to_all x1, waiting for transfers between devices, body(): lax.all_to_all(dqkv_part, 'head', split_axis=0, concat_axis=1, tiled=True)  37.8 us
    reduce_scatter x1, waiting for transfers between devices, body(): lax.psum_scatter(full_qkv.astype(jnp.bfloat16), 'head', scatter_dimension...  37 us
    all_to_all x1, waiting for transfers between devices, body(): lax.all_to_all(qkv_node.reshape(rows, groups, 3 * span), 'head', split_ax...  34.4 us
    reshape x8, local copies, waits for them, and re-layouts, key_sets(): near_kv = kv_all[ids].reshape(GB, NBR * block_size, 2 * span)  33.2 us
  transfers between devices with their start and end apart: 10, of which 9 were waited for; matrix products, arithmetic and copies ran while one was open for 8% of the time, Pallas kernels for 0%

commit v1 on v0

v1 whole, which is shorter than its diff:
```python
import jax
import jax.numpy as jnp
from jax import lax
from jax.experimental import pallas as pl
from jax.experimental.pallas import tpu as pltpu
from jax.sharding import PartitionSpec as P

H = 8
NBR = 4
F32 = jnp.float32
BF16 = jnp.bfloat16


def attention_kernel(near_ref, q_ref, c_ref, kv_ref, far_ref, tile_ref,
                     att_ref, dq_ref, dnear_ref, dfar_ref, acc_ref, bias_ref):
    step = pl.program_id(0)
    block_size, width = q_ref.shape[1], q_ref.shape[2]
    head_dim = width // H
    pair = 2 * head_dim
    reach = (NBR + 1) * block_size
    scale = head_dim ** (-0.5)

    @pl.when(step == 0)
    def _():
        acc_ref[...] = jnp.zeros_like(acc_ref)

    for j in range(NBR):
        bias_ref[:, j * block_size:(j + 1) * block_size] = jnp.where(tile_ref[0, j] != 0, 0.0, -1e30).astype(F32)
    bias_ref[:, NBR * block_size:] = jnp.zeros((block_size, block_size), F32)
    ids = [near_ref[step * NBR + j] for j in range(NBR)]
    first = lax.broadcasted_iota(jnp.int32, (block_size, pair), 1) < head_dim

    def stacked(x):
        zero = jnp.zeros_like(x)
        return jnp.concatenate([jnp.where(first, x, zero), jnp.where(first, zero, x)], axis=0)

    def joined(column):
        cols = pl.ds(column, pair)
        return jnp.concatenate([kv_ref[i, :, cols] for i in ids] + [far_ref[0, :, cols]], axis=0)

    last = (((1,), (1,)), ((), ()))
    lead = (((0,), (0,)), ((), ()))
    for p in range(H // 2):
        low = p * pair
        cols = slice(low, low + pair)
        query = stacked(q_ref[0, :, cols].astype(F32) * scale).astype(BF16)
        cot_pair = c_ref[0, :, cols].astype(F32)
        cot32 = stacked(cot_pair)
        cot = cot32.astype(BF16)
        keys = joined(low)
        values = joined(width + low)
        scores = lax.dot_general(query, keys, last, preferred_element_type=F32)
        bias = bias_ref[...]
        scores = scores + jnp.concatenate([bias, bias], axis=0)
        peak = jnp.max(scores, axis=-1, keepdims=True)
        weight = jnp.exp(scores - peak)
        total = jnp.sum(weight, axis=-1, keepdims=True)
        probs = weight * (1.0 / total)
        low_probs = probs.astype(BF16)
        att2 = jnp.dot(low_probs, values, preferred_element_type=F32).astype(BF16).astype(F32)
        att_ref[0, :, cols] = jnp.where(first, att2[:block_size], att2[block_size:]).astype(BF16)
        delta = jnp.sum(cot32 * att2, axis=-1, keepdims=True)
        grad_probs = lax.dot_general(cot, values, last, preferred_element_type=F32)
        dscores = (probs * (grad_probs - delta)).astype(BF16)
        dq2 = jnp.dot(dscores, keys, preferred_element_type=F32) * scale
        dq_ref[0, :, cols] = jnp.where(first, dq2[:block_size], dq2[block_size:]).astype(BF16)
        dk = lax.dot_general(query, dscores, lead, preferred_element_type=F32)
        dv = lax.dot_general(cot, low_probs, lead, preferred_element_type=F32)
        for base, grad in ((low, dk), (width + low, dv)):
            rows = pl.ds(base, pair)
            for j in range(NBR):
                acc_ref[ids[j], rows, :] += grad[:, j * block_size:(j + 1) * block_size]
            dfar_ref[0, rows, :] = grad[:, NBR * block_size:].astype(BF16)

    @pl.when(step == pl.num_programs(0) - 1)
    def _():
        dnear_ref[...] = acc_ref[...].astype(BF16)


def attention(near_ids, offset, query, cot, kv, kv_far, tiles):
    own, block_size, width = query.shape
    blocks = kv.shape[0]
    scalars = jnp.concatenate([near_ids.reshape(-1), offset.reshape(1)])
    count = own * NBR
    row = lambda b, s: (b, 0, 0)
    whole = lambda b, s: (0, 0, 0)
    grid_spec = pltpu.PrefetchScalarGridSpec(
        num_scalar_prefetch=1,
        grid=(own,),
        in_specs=[
            pl.BlockSpec((1, block_size, width), row),
            pl.BlockSpec((1, block_size, width), row),
            pl.BlockSpec((blocks, block_size, 2 * width), whole),
            pl.BlockSpec((1, block_size, 2 * width), row),
            pl.BlockSpec((1, NBR, block_size, block_size), lambda b, s: (s[count] + b, 0, 0, 0)),
        ],
        out_specs=[
            pl.BlockSpec((1, block_size, width), row),
            pl.BlockSpec((1, block_size, width), row),
            pl.BlockSpec((blocks, 2 * width, block_size), whole),
            pl.BlockSpec((1, 2 * width, block_size), row),
        ],
        scratch_shapes=[
            pltpu.VMEM((blocks, 2 * width, block_size), F32),
            pltpu.VMEM((block_size, (NBR + 1) * block_size), F32),
        ],
    )
    flops = 12 * own * H * block_size * (NBR + 1) * block_size * (width // H)
    return pl.pallas_call(
        attention_kernel,
        grid_spec=grid_spec,
        out_shape=[
            jax.ShapeDtypeStruct((own, block_size, width), BF16),
            jax.ShapeDtypeStruct((own, block_size, width), BF16),
            jax.ShapeDtypeStruct((blocks, 2 * width, block_size), BF16),
            jax.ShapeDtypeStruct((own, 2 * width, block_size), BF16),
        ],
        compiler_params=pltpu.CompilerParams(vmem_limit_bytes=56 * 1024 * 1024),
        cost_estimate=pl.CostEstimate(
            flops=8 * flops,
            bytes_accessed=20 * own * block_size * width,
            transcendentals=own * H * block_size * (NBR + 1) * block_size,
        ),
        name="attention",
    )(scalars, query, cot, kv, kv_far, tiles)


def body(node_feats, w_qkv, w_out, neighbours, tiles, partner, layer_cot):
    rows, width = node_feats.shape
    parts = lax.axis_size("dom")
    groups = lax.axis_size("head")
    me = lax.axis_index("head")
    blocks = partner.shape[0]
    block_size = tiles.shape[2]
    own = blocks // groups
    half = block_size // 2
    span = width // groups
    slots = (blocks + parts - 2) // (parts - 1)
    swap = [(0, 1), (1, 0)]

    def pick(x, i):
        return lax.dynamic_index_in_dim(x, i, 1, keepdims=False)

    def halves(mine, other):
        both = jnp.stack([mine, other], axis=1)
        flip = jnp.stack([other, mine], axis=1)
        return jnp.where(me == 0, both, flip).reshape(mine.shape[0], block_size, -1)

    target = partner // blocks
    iota = jnp.arange(blocks, dtype=jnp.int32)
    same = target[:, None] == target[None, :]
    earlier = iota[None, :] < iota[:, None]
    lower = partner[None, :] < partner[:, None]
    order = (iota + own * me) % blocks
    send_slot = (target * slots + jnp.sum((same & earlier).astype(jnp.int32), axis=1))[order]
    recv_slot = (target * slots + jnp.sum((same & lower).astype(jnp.int32), axis=1))[order]
    all_slots = jnp.arange(parts * slots, dtype=jnp.int32)
    send_from = jnp.sum(jnp.where(send_slot[None, :] == all_slots[:, None], iota[None, :], 0), axis=1)
    recv_from = jnp.sum(jnp.where(recv_slot[None, :] == all_slots[:, None], iota[None, :], 0), axis=1)

    feats = node_feats.reshape(own, 2, half, width)
    peer_a = lax.ppermute(pick(feats, 1 - me), "head", swap)
    peer_b = lax.ppermute(pick(feats, me), "head", swap)
    half_feats = jnp.concatenate([pick(feats, me), peer_a], axis=0)
    incoming = lax.all_to_all(half_feats[send_from], "dom", split_axis=0, concat_axis=0, tiled=True)
    half_far = incoming[recv_slot]
    other_far = lax.ppermute(half_far[own:], "head", swap)
    feats_far = halves(half_far[:own], other_far)
    feats_peer = halves(peer_a, peer_b)

    w_split = w_qkv.reshape(width, groups, 3, span).transpose(0, 2, 1, 3).reshape(width, 3 * width)
    w_query, w_kv = w_split[:, :width], w_split[:, width:]

    def project(x, w):
        return jnp.dot(x, w, preferred_element_type=F32).astype(BF16)

    query = project(node_feats, w_query).reshape(own, block_size, width)
    cot = project(layer_cot, w_out.T).reshape(own, block_size, width)
    feats_near = jnp.concatenate([node_feats, feats_peer.reshape(rows, width)], axis=0)
    feats_far = feats_far.reshape(rows, width)
    kv = project(feats_near, w_kv).reshape(blocks, block_size, 2 * width)
    kv_far = project(feats_far, w_kv).reshape(own, block_size, 2 * width)
    near_ids = lax.dynamic_slice_in_dim(neighbours, me * own, own, 0)
    near_ids = (near_ids + own * me) % blocks
    attended, dq, dnear, dfar = attention(near_ids, me * own, query, cot, kv, kv_far, tiles)

    attended = attended.reshape(rows, width)
    dq = dq.reshape(rows, width)

    def back(x):
        return jnp.einsum("bcn,dc->bnd", x, w_kv, preferred_element_type=F32)

    far_grad = back(dfar).astype(BF16).reshape(own, 2, half, width)
    far_peer = lax.ppermute(pick(far_grad, 1 - me), "head", swap)
    half_grad = jnp.concatenate([pick(far_grad, me), far_peer], axis=0)
    returned = lax.all_to_all(half_grad[recv_from], "dom", split_axis=0, concat_axis=0, tiled=True)
    returned = returned[send_slot].astype(F32)

    peer_grad = back(dnear[own:]).reshape(own, 2, half, width)
    early = lax.ppermute(pick(peer_grad, 1 - me).astype(BF16), "head", swap)
    late = lax.ppermute((pick(peer_grad, me) + returned[own:]).astype(BF16), "head", swap)

    def rows_in(spec, a, b):
        return jnp.einsum(spec, a, b, preferred_element_type=F32)

    dw_q = rows_in("rd,rc->dc", node_feats, dq)
    dw_kv = rows_in("bnd,bcn->dc", feats_near.reshape(blocks, block_size, width), dnear)
    dw_kv = dw_kv + rows_in("bnd,bcn->dc", feats_far.reshape(own, block_size, width), dfar)
    dw_all = jnp.concatenate([dw_q, dw_kv], axis=1).reshape(width, 3, groups, span)
    dw_out = rows_in("rc,rd->cd", layer_cot, attended).reshape(width, groups, span)

    def group_of(i):
        qkv = lax.dynamic_index_in_dim(dw_all, i, 2, keepdims=False).reshape(width, 3 * span)
        return jnp.concatenate([qkv, lax.dynamic_index_in_dim(dw_out, i, 1, keepdims=False)], axis=1)

    dw_peer = lax.ppermute(group_of(1 - me).astype(BF16), "head", swap)
    dw_mine = (group_of(me) + dw_peer.astype(F32)).astype(BF16)
    dw_parts = lax.all_to_all(
        dw_mine.reshape(parts, width // parts, 4 * span), "dom", split_axis=0, concat_axis=0, tiled=True
    )
    dw_sum = jnp.sum(dw_parts.astype(F32), axis=0)

    layer_out = project(attended, w_out)
    own_grad = (
        jnp.einsum("rc,dc->rd", dq, w_query, preferred_element_type=F32).reshape(own, block_size, width)
        + back(dnear[:own])
    )
    feat_grad = own_grad + halves(returned[:own] + early.astype(F32), late.astype(F32))
    feat_grad = feat_grad.astype(BF16).reshape(rows, width)
    return (layer_out, feat_grad, dw_sum[:, : 3 * span], dw_sum[:, 3 * span:].T)


def solution(mesh):
    placed = (
        P(("dom", "head"), None),
        P(),
        P(),
        P("dom", None),
        P("dom", None, None, None),
        P("dom"),
        P(("dom", "head"), None),
    )
    return jax.shard_map(
        body,
        mesh=mesh,
        in_specs=placed,
        out_specs=(
            P(("dom", "head"), None),
            P(("dom", "head"), None),
            P("dom", "head"),
            P("head", "dom"),
        ),
        check_vma=False,
    )
```

time: 853 us -> 259 us (0.30)
  waiting for transfers between devices: 364 us -> 88.1 us
  local copies, waits for them, and re-layouts: 210 us -> 46.6 us
  matrix products: 131 us -> 34.5 us
  other arithmetic: 69.5 us -> 15.5 us
  Pallas kernels: 0 us -> 37.9 us
  loops' own time: 17 us -> 0 us
  between operations: 14.1 us -> 1.1 us
  starting transfers between devices: 43.6 us -> 34.5 us
    all_to_all x6 -> x3, waiting for transfers between devices: 212 us -> 24.6 us  [the longest x1 24.6 us: body(): lax.all_to_all(half_feats[send_from], 'dom', split_axis=0, concat_axis=0,...]
    unnamed x6 -> x0, waiting for transfers between devices: 115 us -> none
    dot_general x38 -> x13, matrix products: 131 us -> 34.5 us  [the longest x5 13.4 us: project(): return jnp.dot(x, w, preferred_element_type=F32).astype(BF16)]
    ppermute x0 -> x7, waiting for transfers between devices: none -> 63.5 us  [the longest x1 17.1 us: body(): dw_peer = lax.ppermute(group_of(1 - me).astype(BF16), 'head', swap)]
    reshape x17 -> x3, local copies, waits for them, and re-layouts: 61.4 us -> 7.13 us  [the longest x1 5.09 us: body(): jnp.concatenate([dw_q, dw_kv], axis=1).reshape(width, 3, groups, span)]
    pallas_call x0 -> x1, Pallas kernels: none -> 37.9 us  [attention(): pl.pallas_call(attention_kernel, grid_spec=grid_spec, out_shape=[jax.Shap...]
    reduce_scatter x2 -> x0, waiting for transfers between devices: 37 us -> none  [the longest x1 37 us: body(): lax.psum_scatter(full_qkv.astype(jnp.bfloat16), 'head', scatter_dimension...]
    concatenate x13 -> x6, other arithmetic: 35.1 us -> 6.54 us  [the longest x1 2 us: body(): jnp.concatenate([dw_q, dw_kv], axis=1).reshape(width, 3, groups, span)]
  transfers between devices with their start and end apart: 10 -> 10, of which waited for: 9 -> 7; matrix products, arithmetic and copies ran while one was open for 8% -> 29% of each run, Pallas kernels for 0% -> 0%
where the time goes in v1:
time: 259 us; the launch traced here: 258 us
  waiting for transfers between devices  88.1 us (34%)
  local copies, waits for them, and re-layouts  46.6 us (18%)
  Pallas kernels  37.9 us (15%)
  starting transfers between devices  34.5 us (13%)
  matrix products  34.5 us (13%)
  other arithmetic  15.5 us (6%)
    pallas_call x1, Pallas kernels, attention(): pl.pallas_call(attention_kernel, grid_spec=grid_spec, out_shape=[jax.Shap...  37.9 us
    all_to_all x1, waiting for transfers between devices, body(): lax.all_to_all(half_feats[send_from], 'dom', split_axis=0, concat_axis=0,...  24.6 us
    ppermute x1, waiting for transfers between devices, body(): dw_peer = lax.ppermute(group_of(1 - me).astype(BF16), 'head', swap)  17.1 us
    dot_general x5, matrix products, project(): return jnp.dot(x, w, preferred_element_type=F32).astype(BF16)  13.4 us
    ppermute x1, waiting for transfers between devices, body(): far_peer = lax.ppermute(pick(far_grad, 1 - me), 'head', swap)  12.3 us
    ppermute x1, waiting for transfers between devices, body(): peer_a = lax.ppermute(pick(feats, 1 - me), 'head', swap)  10.9 us
    all_to_all x1, starting transfers between devices, body(): lax.all_to_all(half_grad[recv_from], 'dom', split_axis=0, concat_axis=0,...  10.3 us
    dot_general x4, matrix products, rows_in(): return jnp.einsum(spec, a, b, preferred_element_type=F32)  9.5 us
  transfers between devices with their start and end apart: 10, of which 7 were waited for; matrix products, arithmetic and copies ran while one was open for 29% of the time, Pallas kernels for 0%

profile of v1, /device:TPU:0, one launch (start us, length us, event | category | flops | bytes accessed | tf_op | source)
XLA Modules:
  0.0 258.2 jit_solution(9789179528510315284)
XLA Ops:
  0.7 2.2 dynamic-slice_bitcast_fusion.4
  2.9 3.0 %collective-permute-start = (bf16[8,64,512]{2,1,0:T(8,128)(2,1)S(1)}, bf16[8,64,512]{2,1,0:T(8,128)(2,1)S(1)}, u32[]{:S(2)}, u32[]{:S(2)}) collective-permute-start(bf16[8,64,512]{2,1,0:T(8,128)(2,1)S(1)} %get-tuple-element.20), channel_id=1, source_target_pairs={{0,1},{1,0},{2,3},{3,2},{4,5},{5,4},{6,7},{7,6},{8,9},{9,8},{10,11... | collective-permute-start | bytes 1572872 | tf_op jit(solution)/shard_map/ppermute | solution.py:162
  6.9 10.9 %collective-permute-done = bf16[8,64,512]{2,1,0:T(8,128)(2,1)S(1)} collective-permute-done((bf16[8,64,512]{2,1,0:T(8,128)(2,1)S(1)}, bf16[8,64,512]{2,1,0:T(8,128)(2,1)S(1)}, u32[]{:S(2)}, u32[]{:S(2)}) %collective-permute-start) | collective-permute-done | bytes 524320 | tf_op jit(solution)/shard_map/ppermute | solution.py:162
  19.1 2.0 gather_fusion.1
  21.1 6.2 %all-to-all-start = ((bf16[32,64,512]{2,1,0:T(8,128)(2,1)}), bf16[32,64,512]{2,1,0:T(8,128)(2,1)}, u32[]{:S(2)}, u32[]{:S(2)}) async-start(bf16[32,64,512]{2,1,0:T(8,128)(2,1)} %gather_fusion.1), calls=%async_computation | async-start | bytes 4194304 | tf_op jit(solution)/shard_map/all_to_all | solution.py:165
  27.3 1.6 collective-permute-start.1
  29.5 2.6 %copy.54 = bf16[512,1536]{0,1:T(8,128)(2,1)} copy(bf16[512,1536]{1,0:T(8,128)(2,1)} %param.8) | data formatting | bytes 3145728 | tf_op args[1]
  32.2 3.9 %copy.55 = bf16[512,3,2,256]{3,2,1,0:T(2,128)(2,1)S(1)} copy(bf16[512,3,2,256]{0,3,1,2:T(8,128)(2,1)} %bitcast.117) | data formatting | bytes 3145728 | tf_op jit(solution)/shard_map/transpose | solution.py:171
  36.1 2.0 reshape.202
  39.0 3.0 %convolution_convert_fusion.5 = bf16[1024,512]{1,0:T(8,128)(2,1)} fusion(bf16[1024,512]{1,0:T(8,128)(2,1)} %param.7, bf16[512,1536]{1,0:T(8,128)(2,1)} %reshape.202), kind=kOutput, calls=%fused_computation.20 | convolution fusion | flops 537395200 | bytes 2621440 | tf_op jit(solution)/shard_map/dot_general | solution.py:175
  42.0 1.7 convolution_convert_fusion.4
  43.7 24.6 %all-to-all-done = bf16[32,64,512]{2,1,0:T(8,128)(2,1)} async-done(((bf16[32,64,512]{2,1,0:T(8,128)(2,1)}), bf16[32,64,512]{2,1,0:T(8,128)(2,1)}, u32[]{:S(2)}, u32[]{:S(2)}) %all-to-all-start) | async-done | bytes 2097184 | tf_op jit(solution)/shard_map/all_to_all | solution.py:165
  68.3 2.2 gather_fusion.3
  70.7 1.6 collective-permute-start.2
  73.1 1.7 maximum_select_fusion.1
  74.8 4.4 %convolution_convert_fusion = bf16[2048,1024]{1,0:T(8,128)(2,1)} fusion(bf16[512,1536]{1,0:T(8,128)(2,1)S(1)} %copy-done.4, bf16[1024,512]{1,0:T(8,128)(2,1)S(1)} %bitcast.119, bf16[1024,512]{1,0:T(8,128)(2,1)S(1)} %copy-done.2), kind=kOutput, calls=%fused_computation.6 | convolution fusion | flops 2153775104 | bytes 7340032 | tf_op jit(solution)/shard_map/dot_general | solution.py:175
  79.2 6.3 %collective-permute-done.2 = bf16[8,64,512]{2,1,0:T(8,128)(2,1)S(1)} collective-permute-done((bf16[8,64,512]{2,1,0:T(8,128)(2,1)S(1)}, bf16[8,64,512]{2,1,0:T(8,128)(2,1)S(1)}, u32[]{:S(2)}, u32[]{:S(2)}) %collective-permute-start.2) | collective-permute-done | bytes 524320 | tf_op jit(solution)/shard_map/ppermute | solution.py:167
  85.6 2.6 %convolution_convert_fusion.1 = bf16[1024,1024]{1,0:T(8,128)(2,1)} fusion(bf16[1024,512]{1,0:T(8,128)(2,1)S(1)} %bitcast.127, bf16[512,1536]{1,0:T(8,128)(2,1)S(1)} %copy-done.4), kind=kOutput, calls=%fused_computation.16 | convolution fusion | flops 1074790400 | bytes 4194304 | tf_op jit(solution)/shard_map/dot_general | solution.py:175
  88.2 37.9 %attention.1 = (bf16[8,128,512]{2,1,0:T(8,128)(2,1)}, bf16[8,128,512]{2,1,0:T(8,128)(2,1)}, bf16[16,1024,128]{2,1,0:T(8,128)(2,1)}, bf16[8,1024,128]{2,1,0:T(8,128)(2,1)}) custom-call(s32[33]{0:T(128)} %pad_add_fusion.near_ref, bf16[8,128,512]{2,1,0:T(8,128)(2,1)} %bitcast.140, bf16[8,128,512]{2,1,0:T(8,128)(2,1)} %bitcast.141, ...), custom_call_target="tpu_custom_call" | custom-call | flops 32212254720 | bytes 10485760 | tf_op jit(solution)/shard_map/attention/pallas_call | solution.py:109
  126.1 2.9 %convolution_convert_fusion.2 = bf16[8,128,512]{2,1,0:T(8,128)(2,1)S(1)} fusion(bf16[8,1024,128]{2,1,0:T(8,128)(2,1)} %get-tuple-element.11, bf16[512,1536]{1,0:T(8,128)(2,1)S(1)} %copy-done.4), kind=kOutput, calls=%fused_computation.17 | convolution fusion | flops 1074266112 | bytes 4194304 | tf_op jit(solution)/shard_map/bcn,dc->bnd/dot_general | solution.py:191
  129.1 1.6 collective-permute-start.3
  130.8 12.3 %collective-permute-done.3 = bf16[8,64,512]{2,1,0:T(8,128)(2,1)S(1)} collective-permute-done((bf16[8,64,512]{2,1,0:T(8,128)(2,1)S(1)}, bf16[8,64,512]{2,1,0:T(8,128)(2,1)S(1)}, u32[]{:S(2)}, u32[]{:S(2)}) %collective-permute-start.3) | collective-permute-done | bytes 524320 | tf_op jit(solution)/shard_map/ppermute | solution.py:194
  143.2 2.0 gather_fusion.4
  145.2 10.3 %all-to-all-start.1 = ((bf16[32,64,512]{2,1,0:T(8,128)(2,1)}), bf16[32,64,512]{2,1,0:T(8,128)(2,1)}, u32[]{:S(2)}, u32[]{:S(2)}) async-start(bf16[32,64,512]{2,1,0:T(8,128)(2,1)} %gather_fusion.4), calls=%async_computation.1 | async-start | bytes 4194304 | tf_op jit(solution)/shard_map/all_to_all | solution.py:196
  155.5 1.5 pad_maximum_fusion.1
  158.2 5.4 %fusion.27 = f32[512,1024,1]{1,0,2:T(8,128)S(1)} fusion(bf16[16,128,512]{2,1,0:T(8,128)(2,1)} %bitcast.123, bf16[16,1024,128]{2,1,0:T(8,128)(2,1)} %get-tuple-element.10), kind=kOutput, calls=%fused_computation.99 | convolution fusion | flops 2147483648 | bytes 8388608 | tf_op jit(solution)/shard_map/bnd,bcn->dc/dot_general | solution.py:204
  164.8 2.0 pad_maximum_fusion
  166.9 5.1 %reshape.214 = f32[512,3,2,256]{3,2,1,0:T(2,128)} reshape(f32[512,1536]{1,0:T(8,128)} %pad_maximum_fusion) | data formatting | bytes 6291456 | tf_op jit(solution)/shard_map/reshape | solution.py:209
  171.9 3.3 %constant_dynamic-slice_fusion = bf16[512,3,1,256]{3,2,1,0:T(2,128)(2,1)S(1)} fusion(f32[512,3,2,256]{3,2,1,0:T(2,128)} %reshape.214, s32[]{:T(128)S(6)} %select_n.142), kind=kLoop, calls=%fused_computation.78 | loop fusion | bytes 1572868 | tf_op jit(solution)/shard_map/jit(dynamic_index_in_dim)/dynamic_slice | solution.py:213
  175.2 2.0 copy.79
  177.2 2.1 fusion.28
  181.4 1.5 collective-permute-start.6
  182.9 2.5 constant_dynamic-slice_fusion.1
  185.4 3.5 %copy.65 = f32[512,3,1,256]{0,3,1,2:T(8,128)S(1)} copy(f32[512,3,1,256]{3,2,1,0:T(1,128)} %constant_dynamic-slice_fusion.1) | data formatting | bytes 3145728 | tf_op jit(solution)/shard_map/jit(dynamic_index_in_dim)/dynamic_slice | solution.py:213
  190.0 17.1 %collective-permute-done.6 = bf16[512,1024]{0,1:T(8,128)(2,1)} collective-permute-done((bf16[512,1024]{0,1:T(8,128)(2,1)}, bf16[512,1024]{0,1:T(8,128)(2,1)}, u32[]{:S(2)}, u32[]{:S(2)}) %collective-permute-start.6) | collective-permute-done | bytes 1048608 | tf_op jit(solution)/shard_map/ppermute | solution.py:216
  207.1 2.6 fusion
  209.7 2.3 copy.69
  212.0 5.7 %all-to-all-start.2 = ((bf16[16,32,1024]{2,1,0:T(8,128)(2,1)}), bf16[16,32,1024]{2,1,0:T(8,128)(2,1)S(1)}, u32[]{:S(2)}, u32[]{:S(2)}) async-start(bf16[16,32,1024]{2,1,0:T(8,128)(2,1)} %bitcast.52), calls=%async_computation.2 | async-start | bytes 2097152 | tf_op jit(solution)/shard_map/all_to_all | solution.py:218
  217.7 3.3 %fusion.4 = f32[8,128,512]{2,1,0:T(8,128)S(1)} fusion(bf16[16,1024,128]{2,1,0:T(8,128)(2,1)} %get-tuple-element.10, bf16[512,1536]{1,0:T(8,128)(2,1)} %reshape.202), kind=kOutput, calls=%fused_computation.32 | convolution fusion | flops 1073741824 | bytes 7340032 | tf_op jit(solution)/shard_map/bcn,dc->bnd/dot_general | solution.py:191
  222.0 1.5 collective-permute-start.4
  223.5 2.6 %fusion.7 = f32[8,128,512]{2,1,0:T(8,128)} fusion(bf16[16,1024,128]{2,1,0:T(8,128)(2,1)S(1)} %copy-done.21, bf16[512,1536]{1,0:T(8,128)(2,1)S(1)} %copy-done.5), kind=kOutput, calls=%fused_computation.35 | convolution fusion | flops 1073741824 | bytes 7340032 | tf_op jit(solution)/shard_map/bcn,dc->bnd/dot_general | solution.py:191
  226.2 2.2 gather_fusion.5
  228.7 7.8 %collective-permute-done.4 = bf16[8,64,512]{2,1,0:T(8,128)(2,1)} collective-permute-done((bf16[8,64,512]{2,1,0:T(8,128)(2,1)}, bf16[8,64,512]{2,1,0:T(8,128)(2,1)}, u32[]{:S(2)}, u32[]{:S(2)}) %collective-permute-start.4) | collective-permute-done | bytes 524320 | tf_op jit(solution)/shard_map/ppermute | solution.py:200
  236.5 2.2 fusion.3
  238.7 1.5 collective-permute-start.5
  240.2 1.7 convolution_convert_fusion.3
  243.4 9.0 %collective-permute-done.5 = bf16[8,64,512]{2,1,0:T(8,128)(2,1)} collective-permute-done((bf16[8,64,512]{2,1,0:T(8,128)(2,1)}, bf16[8,64,512]{2,1,0:T(8,128)(2,1)}, u32[]{:S(2)}, u32[]{:S(2)}) %collective-permute-start.5) | collective-permute-done | bytes 524320 | tf_op jit(solution)/shard_map/ppermute | solution.py:201
  255.4 2.8 %fusion.1 = bf16[8,128,512]{2,1,0:T(8,128)(2,1)} fusion(f32[8,2,64,512]{3,2,1,0:T(8,128)S(1)} %maximum_select_fusion, f32[8,128,512]{2,1,0:T(8,128)S(1)} %copy-done.6, bf16[8,128,512]{2,1,0:T(8,128)(2,1)S(1)} %copy-done.13, bf16[512,1536]{1,0:T(8,128)(2,1)} %reshape.202), kind=kOutput, calls=%fused_computation.14 | convolution fusion | flops 538443776 | bytes 6815744 | tf_op jit(solution)/shard_map/rc,dc->rd/dot_general | solution.py:225
  (88 shorter events, 16.5 us)
Async XLA Ops:
  0.6 41.4 %copy-start = (bf16[1024,512]{1,0:T(8,128)(2,1)S(1)}, bf16[1024,512]{1,0:T(8,128)(2,1)}, u32[]{:S(2)}) copy-start(bf16[1024,512]{1,0:T(8,128)(2,1)} %param.13) | copy-start | bytes 3145732
  0.6 5.2 %copy-start.16 = (s32[16]{0:T(128)S(1)}, s32[16]{0:T(128)}, u32[]{:S(2)}) copy-start(s32[16]{0:T(128)} %param.12) | copy-start | bytes 196
  2.9 14.9 %collective-permute-start = (bf16[8,64,512]{2,1,0:T(8,128)(2,1)S(1)}, bf16[8,64,512]{2,1,0:T(8,128)(2,1)S(1)}, u32[]{:S(2)}, u32[]{:S(2)}) collective-permute-start(bf16[8,64,512]{2,1,0:T(8,128)(2,1)S(1)} %get-tuple-element.20), channel_id=1, source_target_pairs={{0,1},{1,0},{2,3},{3,2},{4,5},{5,4},{6,7},{7,6},{8,9},{9,8},{10,11... | collective-permute-start | bytes 1572872 | tf_op jit(solution)/shard_map/ppermute | solution.py:162
  17.8 3.3 %copy-start.7 = (bf16[8,64,512]{2,1,0:T(8,128)(2,1)}, bf16[8,64,512]{2,1,0:T(8,128)(2,1)S(1)}, u32[]{:S(2)}) copy-start(bf16[8,64,512]{2,1,0:T(8,128)(2,1)S(1)} %collective-permute-done) | copy-start | bytes 1572868
  21.1 47.2 %all-to-all-start = ((bf16[32,64,512]{2,1,0:T(8,128)(2,1)}), bf16[32,64,512]{2,1,0:T(8,128)(2,1)}, u32[]{:S(2)}, u32[]{:S(2)}) async-start(bf16[32,64,512]{2,1,0:T(8,128)(2,1)} %gather_fusion.1), calls=%async_computation | async-start | bytes 4194304 | tf_op jit(solution)/shard_map/all_to_all | solution.py:165
  27.3 44.9 %collective-permute-start.1 = (bf16[8,64,512]{2,1,0:T(8,128)(2,1)}, bf16[8,64,512]{2,1,0:T(8,128)(2,1)S(1)}, u32[]{:S(2)}, u32[]{:S(2)}) collective-permute-start(bf16[8,64,512]{2,1,0:T(8,128)(2,1)} %get-tuple-element.21), channel_id=1, source_target_pairs={{0,1},{1,0},{2,3},{3,2},{4,5},{5,4},{6,7},{7,6},{8,9},{9,8},{10,11... | collective-permute-start | bytes 1572872 | tf_op jit(solution)/shard_map/ppermute | solution.py:163
  36.1 2.0 copy-start.17
  38.1 3.9 %copy-start.18 = (bf16[512,512]{1,0:T(8,128)(2,1)S(1)}, bf16[512,512]{1,0:T(8,128)(2,1)}, u32[]{:S(2)}) copy-start(bf16[512,512]{1,0:T(8,128)(2,1)} %param.9) | copy-start | bytes 1572868
  70.5 4.3 %copy-start.2 = (bf16[1024,512]{1,0:T(8,128)(2,1)S(1)}, bf16[1024,512]{1,0:T(8,128)(2,1)}, u32[]{:S(2)}) copy-start(bf16[1024,512]{1,0:T(8,128)(2,1)} %param.7) | copy-start | bytes 3145732
  70.5 4.3 %copy-start.4 = (bf16[512,1536]{1,0:T(8,128)(2,1)S(1)}, bf16[512,1536]{1,0:T(8,128)(2,1)}, u32[]{:S(2)}) copy-start(bf16[512,1536]{1,0:T(8,128)(2,1)} %reshape.202) | copy-start | bytes 4718596
  70.7 14.9 %collective-permute-start.2 = (bf16[8,64,512]{2,1,0:T(8,128)(2,1)S(1)}, bf16[8,64,512]{2,1,0:T(8,128)(2,1)S(1)}, u32[]{:S(2)}, u32[]{:S(2)}) collective-permute-start(bf16[8,64,512]{2,1,0:T(8,128)(2,1)S(1)} %get-tuple-element.19), channel_id=1, source_target_pairs={{0,1},{1,0},{2,3},{3,2},{4,5},{5,4},{6,7},{7,6},{8,9},{9,8},{10,11... | collective-permute-start | bytes 1572872 | tf_op jit(solution)/shard_map/ppermute | solution.py:167
  72.2 0.8 copy-start.15
  85.6 2.6 %copy-start.10 = (bf16[8,2,64,512]{3,2,1,0:T(8,128)(2,1)}, bf16[8,2,64,512]{3,2,1,0:T(8,128)(2,1)S(1)}, u32[]{:S(2)}) copy-start(bf16[8,2,64,512]{3,2,1,0:T(8,128)(2,1)S(1)} %maximum_select_fusion.2) | copy-start | bytes 3145732
  129.1 14.0 %collective-permute-start.3 = (bf16[8,64,512]{2,1,0:T(8,128)(2,1)S(1)}, bf16[8,64,512]{2,1,0:T(8,128)(2,1)S(1)}, u32[]{:S(2)}, u32[]{:S(2)}) collective-permute-start(bf16[8,64,512]{2,1,0:T(8,128)(2,1)S(1)} %get-tuple-element.17), channel_id=1, source_target_pairs={{0,1},{1,0},{2,3},{3,2},{4,5},{5,4},{6,7},{7,6},{8,9},{9,8},{10,11... | collective-permute-start | bytes 1572872 | tf_op jit(solution)/shard_map/ppermute | solution.py:194
  145.2 10.3 %copy-start.3 = (bf16[1024,512]{1,0:T(8,128)(2,1)S(1)}, bf16[1024,512]{1,0:T(8,128)(2,1)}, u32[]{:S(2)}) copy-start(bf16[1024,512]{1,0:T(8,128)(2,1)} %param.7) | copy-start | bytes 3145732
  145.2 66.8 %all-to-all-start.1 = ((bf16[32,64,512]{2,1,0:T(8,128)(2,1)}), bf16[32,64,512]{2,1,0:T(8,128)(2,1)}, u32[]{:S(2)}, u32[]{:S(2)}) async-start(bf16[32,64,512]{2,1,0:T(8,128)(2,1)} %gather_fusion.4), calls=%async_computation.1 | async-start | bytes 4194304 | tf_op jit(solution)/shard_map/all_to_all | solution.py:196
  155.5 1.6 copy-start.12
  158.1 5.4 %copy-start.11 = (bf16[8,2,64,512]{3,2,1,0:T(8,128)(2,1)S(1)}, bf16[8,2,64,512]{3,2,1,0:T(8,128)(2,1)}, u32[]{:S(2)}) copy-start(bf16[8,2,64,512]{3,2,1,0:T(8,128)(2,1)} %copy-done.10) | copy-start | bytes 3145732
  158.2 5.4 %copy-start.22 = (bf16[8,1024,128]{2,1,0:T(8,128)(2,1)S(1)}, bf16[8,1024,128]{2,1,0:T(8,128)(2,1)}, u32[]{:S(2)}) copy-start(bf16[8,1024,128]{2,1,0:T(8,128)(2,1)} %get-tuple-element.11) | copy-start | bytes 6291460
  177.2 5.7 %copy-start.1 = (f32[512,3,2,256]{3,2,1,0:T(2,128)S(1)}, f32[512,3,2,256]{3,2,1,0:T(2,128)}, u32[]{:S(2)}) copy-start(f32[512,3,2,256]{3,2,1,0:T(2,128)} %reshape.214) | copy-start | bytes 9437188
  179.3 1.0 copy-start.14
  181.4 25.7 %collective-permute-start.6 = (bf16[512,1024]{0,1:T(8,128)(2,1)}, bf16[512,1024]{0,1:T(8,128)(2,1)}, u32[]{:S(2)}, u32[]{:S(2)}) collective-permute-start(bf16[512,1024]{0,1:T(8,128)(2,1)} %pad_maximum_fusion.4), channel_id=1, source_target_pairs={{0,1},{1,0},{2,3},{3,2},{4,5},{5,4},{6,7},{7,6},{8,9},{9,8},{10,11... | collective-permute-start | bytes 3145736 | tf_op jit(solution)/shard_map/ppermute | solution.py:216
  212.0 29.9 %all-to-all-start.2 = ((bf16[16,32,1024]{2,1,0:T(8,128)(2,1)}), bf16[16,32,1024]{2,1,0:T(8,128)(2,1)S(1)}, u32[]{:S(2)}, u32[]{:S(2)}) async-start(bf16[16,32,1024]{2,1,0:T(8,128)(2,1)} %bitcast.52), calls=%async_computation.2 | async-start | bytes 2097152 | tf_op jit(solution)/shard_map/all_to_all | solution.py:218
  217.7 5.8 %copy-start.5 = (bf16[512,1536]{1,0:T(8,128)(2,1)S(1)}, bf16[512,1536]{1,0:T(8,128)(2,1)}, u32[]{:S(2)}) copy-start(bf16[512,1536]{1,0:T(8,128)(2,1)} %reshape.202) | copy-start | bytes 4718596
  217.7 5.8 %copy-start.21 = (bf16[16,1024,128]{2,1,0:T(8,128)(2,1)S(1)}, bf16[16,1024,128]{2,1,0:T(8,128)(2,1)}, u32[]{:S(2)}) copy-start(bf16[16,1024,128]{2,1,0:T(8,128)(2,1)} %get-tuple-element.10) | copy-start | bytes 12582916
  221.0 2.5 copy-start.8
  222.0 14.5 %collective-permute-start.4 = (bf16[8,64,512]{2,1,0:T(8,128)(2,1)}, bf16[8,64,512]{2,1,0:T(8,128)(2,1)}, u32[]{:S(2)}, u32[]{:S(2)}) collective-permute-start(bf16[8,64,512]{2,1,0:T(8,128)(2,1)} %fusion.14), channel_id=1, source_target_pairs={{0,1},{1,0},{2,3},{3,2},{4,5},{5,4},{6,7},{7,6},{8,9},{9,8},{10,11... | collective-permute-start | bytes 1572872 | tf_op jit(solution)/shard_map/ppermute | solution.py:200
  228.4 8.1 %copy-start.9 = (f32[8,128,512]{2,1,0:T(8,128)S(1)}, f32[8,128,512]{2,1,0:T(8,128)}, u32[]{:S(2)}) copy-start(f32[8,128,512]{2,1,0:T(8,128)} %copy-done.8) | copy-start | bytes 6291460
  228.7 11.5 %copy-start.19 = (bf16[512,512]{1,0:T(8,128)(2,1)S(1)}, bf16[512,512]{1,0:T(8,128)(2,1)}, u32[]{:S(2)}) copy-start(bf16[512,512]{1,0:T(8,128)(2,1)} %param.9) | copy-start | bytes 1572868
  228.7 11.5 %copy-start.20 = (bf16[8,128,512]{2,1,0:T(8,128)(2,1)S(1)}, bf16[8,128,512]{2,1,0:T(8,128)(2,1)}, u32[]{:S(2)}) copy-start(bf16[8,128,512]{2,1,0:T(8,128)(2,1)} %get-tuple-element.8) | copy-start | bytes 3145732
  238.7 13.7 %collective-permute-start.5 = (bf16[8,64,512]{2,1,0:T(8,128)(2,1)}, bf16[8,64,512]{2,1,0:T(8,128)(2,1)}, u32[]{:S(2)}, u32[]{:S(2)}) collective-permute-start(bf16[8,64,512]{2,1,0:T(8,128)(2,1)} %get-tuple-element.15), channel_id=1, source_target_pairs={{0,1},{1,0},{2,3},{3,2},{4,5},{5,4},{6,7},{7,6},{8,9},{9,8},{10,11... | collective-permute-start | bytes 1572872 | tf_op jit(solution)/shard_map/ppermute | solution.py:201
  253.6 1.6 copy-start.6
  253.6 1.9 copy-start.13

commit v2 on v1

--- a/solution.py
+++ b/solution.py
@@ -190,33 +190,48 @@
     def back(x):
         return jnp.einsum("bcn,dc->bnd", x, w_kv, preferred_element_type=F32)
 
+    core = lax.axis_index("dom") % 2
+    chip_swap = [(i, i ^ 1) for i in range(parts)]
+    same_core = [[i for i in range(parts) if i % 2 == c] for c in range(2)]
+
+    def rows_in(spec, a, b):
+        return jnp.einsum(spec, a, b, preferred_element_type=F32)
+
+    near_rows = feats_near.reshape(blocks, block_size, width)
+    far_rows = feats_far.reshape(own, block_size, width)
+    near_split = dnear.reshape(blocks, 2, groups, span, block_size)
+    far_split = dfar.reshape(own, 2, groups, span, block_size)
+
+    def group_of(i):
+        cols = lambda x: lax.dynamic_slice_in_dim(x, i * span, span, 1)
+        dw_q = rows_in("rd,rc->dc", node_feats, cols(dq))
+        near = lax.dynamic_index_in_dim(near_split, i, 2, keepdims=False).reshape(blocks, 2 * span, block_size)
+        far = lax.dynamic_index_in_dim(far_split, i, 2, keepdims=False).reshape(own, 2 * span, block_size)
+        dw_kv = rows_in("bnd,bcn->dc", near_rows, near) + rows_in("bnd,bcn->dc", far_rows, far)
+        dw_out = rows_in("rc,rd->cd", layer_cot, cols(attended))
+        return dw_q, dw_kv, dw_out
+
     far_grad = back(dfar).astype(BF16).reshape(own, 2, half, width)
     far_peer = lax.ppermute(pick(far_grad, 1 - me), "head", swap)
+    dw_send = jnp.concatenate([x.astype(BF16) for x in group_of(1 - me)], axis=1)
+    peer_grad = back(dnear[own:]).reshape(own, 2, half, width)
+    early_send = pick(peer_grad, 1 - me).astype(BF16)
+    far_peer, dw_send, early_send = lax.optimization_barrier((far_peer, dw_send, early_send))
     half_grad = jnp.concatenate([pick(far_grad, me), far_peer], axis=0)
     returned = lax.all_to_all(half_grad[recv_from], "dom", split_axis=0, concat_axis=0, tiled=True)
+    dw_peer = lax.ppermute(dw_send, "head", swap)
+    early = lax.ppermute(early_send, "head", swap)
+
+    dw_mine = jnp.concatenate(group_of(me), axis=1) + dw_peer.astype(F32)
+    dw_mine = dw_mine.reshape(parts // 2, 2, width // parts, 4 * span)
+    dw_core = lax.ppermute(pick(dw_mine, 1 - core).astype(BF16), "dom", chip_swap)
+    dw_half = (pick(dw_mine, core) + dw_core.astype(F32)).astype(BF16)
+    returned, dw_half = lax.optimization_barrier((returned, dw_half))
+
     returned = returned[send_slot].astype(F32)
-
-    peer_grad = back(dnear[own:]).reshape(own, 2, half, width)
-    early = lax.ppermute(pick(peer_grad, 1 - me).astype(BF16), "head", swap)
     late = lax.ppermute((pick(peer_grad, me) + returned[own:]).astype(BF16), "head", swap)
-
-    def rows_in(spec, a, b):
-        return jnp.einsum(spec, a, b, preferred_element_type=F32)
-
-    dw_q = rows_in("rd,rc->dc", node_feats, dq)
-    dw_kv = rows_in("bnd,bcn->dc", feats_near.reshape(blocks, block_size, width), dnear)
-    dw_kv = dw_kv + rows_in("bnd,bcn->dc", feats_far.reshape(own, block_size, width), dfar)
-    dw_all = jnp.concatenate([dw_q, dw_kv], axis=1).reshape(width, 3, groups, span)
-    dw_out = rows_in("rc,rd->cd", layer_cot, attended).reshape(width, groups, span)
-
-    def group_of(i):
-        qkv = lax.dynamic_index_in_dim(dw_all, i, 2, keepdims=False).reshape(width, 3 * span)
-        return jnp.concatenate([qkv, lax.dynamic_index_in_dim(dw_out, i, 1, keepdims=False)], axis=1)
-
-    dw_peer = lax.ppermute(group_of(1 - me).astype(BF16), "head", swap)
-    dw_mine = (group_of(me) + dw_peer.astype(F32)).astype(BF16)
     dw_parts = lax.all_to_all(
-        dw_mine.reshape(parts, width // parts, 4 * span), "dom", split_axis=0, concat_axis=0, tiled=True
+        dw_half, "dom", split_axis=0, concat_axis=0, tiled=True, axis_index_groups=same_core
     )
     dw_sum = jnp.sum(dw_parts.astype(F32), axis=0)
 

time: 259 us -> 241 us (0.931)
  waiting for transfers between devices: 88.1 us -> 79 us
  local copies, waits for them, and re-layouts: 46.6 us -> 39.8 us
  matrix products: 34.5 us -> 31.2 us
  starting transfers between devices: 34.5 us -> 37.7 us
    ppermute x1, waiting for transfers between devices: 9.02 us -> 0.01 us  [body(): lax.ppermute((pick(peer_grad, me) + returned[own:]).astype(BF16), 'head',...]
    dynamic_slice x3 -> x2, local copies, waits for them, and re-layouts: 9.29 us -> 2.97 us  [the longest x1 1.82 us: group_of(): lax.dynamic_index_in_dim(near_split, i, 2, keepdims=False)]
    all_to_all x1, waiting for transfers between devices: 0.01 us -> 6.08 us  [body(): lax.all_to_all(dw_half, 'dom', split_axis=0, concat_axis=0, tiled=True, a...]
    all_to_all x1, waiting for transfers between devices: 24.6 us -> 19.2 us  [body(): lax.all_to_all(half_feats[send_from], 'dom', split_axis=0, concat_axis=0,...]
    all_to_all x1, waiting for transfers between devices: 0.01 us -> 5.16 us  [body(): lax.all_to_all(half_grad[recv_from], 'dom', split_axis=0, concat_axis=0,...]
    reshape x1 -> x0, local copies, waits for them, and re-layouts: 5.09 us -> none  [body(): jnp.concatenate([dw_q, dw_kv], axis=1).reshape(width, 3, groups, span)]
    ppermute x2 -> x3, waiting for transfers between devices: 24.9 us -> 21.5 us  [the longest x1 18.6 us: body(): dw_peer = lax.ppermute(dw_send, 'head', swap)]
    reshape x1, local copies, waits for them, and re-layouts: 1.96 us -> 4.97 us  [body(): w_qkv.reshape(width, groups, 3, span).transpose(0, 2, 1, 3)]
  transfers between devices with their start and end apart: 10 -> 11, of which waited for: 7 -> 9; matrix products, arithmetic and copies ran while one was open for 29% -> 22% of each run, Pallas kernels for 0% -> 0%
where the time goes in v2:
time: 241 us; the launch traced here: 240 us
  waiting for transfers between devices  79 us (33%)
  local copies, waits for them, and re-layouts  39.8 us (17%)
  Pallas kernels  37.9 us (16%)
  starting transfers between devices  37.7 us (16%)
  matrix products  31.2 us (13%)
  other arithmetic  13.3 us (6%)
    pallas_call x1, Pallas kernels, attention(): pl.pallas_call(attention_kernel, grid_spec=grid_spec, out_shape=[jax.Shap...  37.9 us
    all_to_all x1, waiting for transfers between devices, body(): lax.all_to_all(half_feats[send_from], 'dom', split_axis=0, concat_axis=0,...  19.2 us
    ppermute x1, waiting for transfers between devices, body(): dw_peer = lax.ppermute(dw_send, 'head', swap)  18.6 us
    dot_general x5, matrix products, project(): return jnp.dot(x, w, preferred_element_type=F32).astype(BF16)  14.3 us
    all_to_all x1, starting transfers between devices, body(): lax.all_to_all(half_grad[recv_from], 'dom', split_axis=0, concat_axis=0,...  10.3 us
    ppermute x1, waiting for transfers between devices, body(): peer_a = lax.ppermute(pick(feats, 1 - me), 'head', swap)  10.2 us
    ppermute x1, waiting for transfers between devices, body(): far_peer = lax.ppermute(pick(far_grad, 1 - me), 'head', swap)  9.39 us
    unnamed x51, local copies, waits for them, and re-layouts  8.99 us
  transfers between devices with their start and end apart: 11, of which 9 were waited for; matrix products, arithmetic and copies ran while one was open for 22% of the time, Pallas kernels for 0%

profile of v2, /device:TPU:0, one launch (start us, length us, event | category | flops | bytes accessed | tf_op | source)
XLA Modules:
  0.0 240.0 jit_solution(14587476101699067220)
XLA Ops:
  0.7 1.4 dynamic-slice_bitcast_fusion.3
  2.1 3.1 %collective-permute-start = (bf16[8,64,512]{2,1,0:T(8,128)(2,1)S(1)}, bf16[8,64,512]{2,1,0:T(8,128)(2,1)S(1)}, u32[]{:S(2)}, u32[]{:S(2)}) collective-permute-start(bf16[8,64,512]{2,1,0:T(8,128)(2,1)S(1)} %get-tuple-element.34), channel_id=1, source_target_pairs={{0,1},{1,0},{2,3},{3,2},{4,5},{5,4},{6,7},{7,6},{8,9},{9,8},{10,11... | collective-permute-start | bytes 1572872 | tf_op jit(solution)/shard_map/ppermute | solution.py:162
  6.8 10.2 %collective-permute-done = bf16[8,64,512]{2,1,0:T(8,128)(2,1)S(1)} collective-permute-done((bf16[8,64,512]{2,1,0:T(8,128)(2,1)S(1)}, bf16[8,64,512]{2,1,0:T(8,128)(2,1)S(1)}, u32[]{:S(2)}, u32[]{:S(2)}) %collective-permute-start) | collective-permute-done | bytes 524320 | tf_op jit(solution)/shard_map/ppermute | solution.py:162
  17.1 2.0 gather_fusion.1
  19.1 6.2 %all-to-all-start = ((bf16[32,64,512]{2,1,0:T(8,128)(2,1)}), bf16[32,64,512]{2,1,0:T(8,128)(2,1)}, u32[]{:S(2)}, u32[]{:S(2)}) async-start(bf16[32,64,512]{2,1,0:T(8,128)(2,1)} %gather_fusion.1), calls=%async_computation | async-start | bytes 4194304 | tf_op jit(solution)/shard_map/all_to_all | solution.py:165
  25.3 1.6 collective-permute-start.1
  26.9 2.6 %copy.26 = bf16[512,1536]{0,1:T(8,128)(2,1)} copy(bf16[512,1536]{1,0:T(8,128)(2,1)} %param.8) | data formatting | bytes 3145728 | tf_op args[1]
  29.5 5.0 %copy.27 = bf16[512,3,2,256]{3,2,1,0:T(2,128)(2,1)} copy(bf16[512,3,2,256]{0,3,1,2:T(8,128)(2,1)} %bitcast.138) | data formatting | bytes 3145728 | tf_op jit(solution)/shard_map/transpose | solution.py:171
  34.5 5.0 %reshape.222 = bf16[512,1536]{1,0:T(8,128)(2,1)} reshape(bf16[512,3,2,256]{3,2,1,0:T(2,128)(2,1)} %copy.27) | data formatting | bytes 3145728 | tf_op jit(solution)/shard_map/reshape | solution.py:171
  40.4 2.7 %convolution_convert_fusion.5 = bf16[1024,512]{1,0:T(8,128)(2,1)} fusion(bf16[1024,512]{1,0:T(8,128)(2,1)S(1)} %copy-done.1, bf16[512,1536]{1,0:T(8,128)(2,1)} %reshape.222), kind=kOutput, calls=%fused_computation.16 | convolution fusion | flops 537395200 | bytes 2621440 | tf_op jit(solution)/shard_map/dot_general | solution.py:175
  43.1 1.7 convolution_convert_fusion.4
  44.8 2.4 maximum_select_fusion.1
  47.2 19.2 %all-to-all-done = bf16[32,64,512]{2,1,0:T(8,128)(2,1)} async-done(((bf16[32,64,512]{2,1,0:T(8,128)(2,1)}), bf16[32,64,512]{2,1,0:T(8,128)(2,1)}, u32[]{:S(2)}, u32[]{:S(2)}) %all-to-all-start) | async-done | bytes 2097184 | tf_op jit(solution)/shard_map/all_to_all | solution.py:165
  66.4 2.2 gather_fusion.3
  68.7 1.6 collective-permute-start.2
  70.4 1.3 copy-done.5
  71.7 4.4 %convolution_convert_fusion = bf16[2048,1024]{1,0:T(8,128)(2,1)} fusion(bf16[512,1536]{1,0:T(8,128)(2,1)S(1)} %copy-done.5, bf16[1024,512]{1,0:T(8,128)(2,1)S(1)} %bitcast.141, bf16[1024,512]{1,0:T(8,128)(2,1)S(1)} %copy-done.1), kind=kOutput, calls=%fused_computation.6 | convolution fusion | flops 2153775104 | bytes 7340032 | tf_op jit(solution)/shard_map/dot_general | solution.py:175
  76.1 7.5 %collective-permute-done.2 = bf16[8,64,512]{2,1,0:T(8,128)(2,1)S(1)} collective-permute-done((bf16[8,64,512]{2,1,0:T(8,128)(2,1)S(1)}, bf16[8,64,512]{2,1,0:T(8,128)(2,1)S(1)}, u32[]{:S(2)}, u32[]{:S(2)}) %collective-permute-start.2) | collective-permute-done | bytes 524320 | tf_op jit(solution)/shard_map/ppermute | solution.py:167
  83.7 2.6 %convolution_convert_fusion.1 = bf16[1024,1024]{1,0:T(8,128)(2,1)} fusion(bf16[1024,512]{1,0:T(8,128)(2,1)S(1)} %bitcast.154, bf16[512,1536]{1,0:T(8,128)(2,1)S(1)} %copy-done.5), kind=kOutput, calls=%fused_computation.12 | convolution fusion | flops 1074790400 | bytes 4194304 | tf_op jit(solution)/shard_map/dot_general | solution.py:175
  86.3 37.9 %attention.1 = (bf16[8,128,512]{2,1,0:T(8,128)(2,1)}, bf16[8,128,512]{2,1,0:T(8,128)(2,1)}, bf16[16,1024,128]{2,1,0:T(8,128)(2,1)}, bf16[8,1024,128]{2,1,0:T(8,128)(2,1)}) custom-call(s32[33]{0:T(128)} %pad_add_fusion.near_ref, bf16[8,128,512]{2,1,0:T(8,128)(2,1)} %bitcast.165, bf16[8,128,512]{2,1,0:T(8,128)(2,1)} %bitcast.166, ...), custom_call_target="tpu_custom_call" | custom-call | flops 32212254720 | bytes 10485760 | tf_op jit(solution)/shard_map/attention/pallas_call | solution.py:109
  124.2 3.0 %convolution_convert_fusion.2 = bf16[8,128,512]{2,1,0:T(8,128)(2,1)S(1)} fusion(bf16[8,1024,128]{2,1,0:T(8,128)(2,1)} %get-tuple-element.16, bf16[512,1536]{1,0:T(8,128)(2,1)S(1)} %copy-done.5), kind=kOutput, calls=%fused_computation.13 | convolution fusion | flops 1074266112 | bytes 4194304 | tf_op jit(solution)/shard_map/bcn,dc->bnd/dot_general | solution.py:191
  128.4 1.4 copy-done.2
  129.8 1.3 fusion.9
  131.1 1.8 constant_dynamic-slice_fusion.1
  135.6 1.6 collective-permute-start.3
  137.9 1.3 fusion.3
  140.2 9.4 %collective-permute-done.3 = bf16[8,64,512]{2,1,0:T(8,128)(2,1)S(1)} collective-permute-done((bf16[8,64,512]{2,1,0:T(8,128)(2,1)S(1)}, bf16[8,64,512]{2,1,0:T(8,128)(2,1)S(1)}, u32[]{:S(2)}, u32[]{:S(2)}) %collective-permute-start.3) | collective-permute-done | bytes 524320 | tf_op jit(solution)/shard_map/ppermute | solution.py:215
  149.7 2.0 gather_fusion.4
  151.7 10.3 %all-to-all-start.1 = ((bf16[32,64,512]{2,1,0:T(8,128)(2,1)}), bf16[32,64,512]{2,1,0:T(8,128)(2,1)}, u32[]{:S(2)}, u32[]{:S(2)}) async-start(bf16[32,64,512]{2,1,0:T(8,128)(2,1)} %gather_fusion.4), calls=%async_computation.1 | async-start | bytes 4194304 | tf_op jit(solution)/shard_map/all_to_all | solution.py:221
  162.0 1.6 collective-permute-start.4
  163.6 2.0 convolution_bitcast_fusion
  167.8 1.2 fusion.2
  169.1 18.6 %collective-permute-done.4 = bf16[512,1024]{0,1:T(8,128)(2,1)S(1)} collective-permute-done((bf16[512,1024]{0,1:T(8,128)(2,1)}, bf16[512,1024]{0,1:T(8,128)(2,1)S(1)}, u32[]{:S(2)}, u32[]{:S(2)}) %collective-permute-start.4) | collective-permute-done | bytes 1048608 | tf_op jit(solution)/shard_map/ppermute | solution.py:222
  187.7 1.7 maximum_add_fusion
  189.4 3.0 %copy.32 = f32[512,1024]{1,0:T(8,128)} copy(f32[512,1024]{0,1:T(8,128)} %maximum_add_fusion) | data formatting | bytes 4194304 | tf_op jit(solution)/shard_map/add | solution.py:225
  192.3 1.3 fusion.19
  193.7 1.6 collective-permute-start.6
  195.6 2.2 fusion.8
  197.8 5.2 %all-to-all-done.1 = bf16[32,64,512]{2,1,0:T(8,128)(2,1)} async-done(((bf16[32,64,512]{2,1,0:T(8,128)(2,1)}), bf16[32,64,512]{2,1,0:T(8,128)(2,1)}, u32[]{:S(2)}, u32[]{:S(2)}) %all-to-all-start.1) | async-done | bytes 2097184 | tf_op jit(solution)/shard_map/all_to_all | solution.py:221
  203.0 2.2 gather_fusion.5
  205.5 2.6 %collective-permute-done.6 = bf16[8,64,512]{2,1,0:T(8,128)(2,1)} collective-permute-done((bf16[8,64,512]{2,1,0:T(8,128)(2,1)S(1)}, bf16[8,64,512]{2,1,0:T(8,128)(2,1)}, u32[]{:S(2)}, u32[]{:S(2)}) %collective-permute-start.6) | collective-permute-done | bytes 524320 | tf_op jit(solution)/shard_map/ppermute | solution.py:223
  208.2 1.7 fusion.7
  209.9 1.6 collective-permute-start.7
  211.5 2.6 %fusion.12 = f32[8,128,512]{2,1,0:T(8,128)} fusion(bf16[16,1024,128]{2,1,0:T(8,128)(2,1)S(1)} %copy-done.3, bf16[512,1536]{1,0:T(8,128)(2,1)S(1)} %copy-done.6), kind=kOutput, calls=%fused_computation.45 | convolution fusion | flops 1073741824 | bytes 7340032 | tf_op jit(solution)/shard_map/bcn,dc->bnd/dot_general | solution.py:191
  214.1 8.6 %all-to-all-start.2 = ((bf16[8,32,1024]{2,1,0:T(8,128)(2,1)}), bf16[8,32,1024]{2,1,0:T(8,128)(2,1)}, u32[]{:S(2)}, u32[]{:S(2)}) async-start(bf16[8,32,1024]{2,1,0:T(8,128)(2,1)} %fusion.8), calls=%async_computation.2 | async-start | bytes 1048576 | tf_op jit(solution)/shard_map/all_to_all | solution.py:233
  222.8 2.9 %convolution_convert_fusion.3 = bf16[1024,512]{1,0:T(8,128)(2,1)} fusion(bf16[1024,512]{1,0:T(8,128)(2,1)} %bitcast.160, bf16[512,512]{1,0:T(8,128)(2,1)S(1)} %copy-done.24), kind=kOutput, calls=%fused_computation.14 | convolution fusion | flops 537395200 | bytes 2621440 | tf_op jit(solution)/shard_map/dot_general | solution.py:175
  228.8 2.8 %fusion = bf16[8,128,512]{2,1,0:T(8,128)(2,1)} fusion(f32[8,2,64,512]{3,2,1,0:T(8,128)S(1)} %maximum_select_fusion, f32[8,128,512]{2,1,0:T(8,128)S(1)} %copy-done.14, bf16[8,128,512]{2,1,0:T(8,128)(2,1)S(1)} %copy-done.9, bf16[512,1536]{1,0:T(8,128)(2,1)} %reshape.222), kind=kOutput, calls=%fused_computation.11 | convolution fusion | flops 538443776 | bytes 6815744 | tf_op jit(solution)/shard_map/rc,dc->rd/dot_general | solution.py:240
  231.6 6.1 %all-to-all-done.2 = bf16[8,32,1024]{2,1,0:T(8,128)(2,1)} async-done(((bf16[8,32,1024]{2,1,0:T(8,128)(2,1)}), bf16[8,32,1024]{2,1,0:T(8,128)(2,1)}, u32[]{:S(2)}, u32[]{:S(2)}) %all-to-all-start.2) | async-done | bytes 524320 | tf_op jit(solution)/shard_map/all_to_all | solution.py:233
  (92 shorter events, 16.9 us)
Async XLA Ops:
  0.6 42.5 %copy-start = (bf16[1024,512]{1,0:T(8,128)(2,1)S(1)}, bf16[1024,512]{1,0:T(8,128)(2,1)}, u32[]{:S(2)}) copy-start(bf16[1024,512]{1,0:T(8,128)(2,1)} %param.13) | copy-start | bytes 3145732
  0.6 4.5 %copy-start.21 = (s32[16]{0:T(128)S(1)}, s32[16]{0:T(128)}, u32[]{:S(2)}) copy-start(s32[16]{0:T(128)} %param.12) | copy-start | bytes 196
  2.1 15.0 %collective-permute-start = (bf16[8,64,512]{2,1,0:T(8,128)(2,1)S(1)}, bf16[8,64,512]{2,1,0:T(8,128)(2,1)S(1)}, u32[]{:S(2)}, u32[]{:S(2)}) collective-permute-start(bf16[8,64,512]{2,1,0:T(8,128)(2,1)S(1)} %get-tuple-element.34), channel_id=1, source_target_pairs={{0,1},{1,0},{2,3},{3,2},{4,5},{5,4},{6,7},{7,6},{8,9},{9,8},{10,11... | collective-permute-start | bytes 1572872 | tf_op jit(solution)/shard_map/ppermute | solution.py:162
  19.1 47.2 %all-to-all-start = ((bf16[32,64,512]{2,1,0:T(8,128)(2,1)}), bf16[32,64,512]{2,1,0:T(8,128)(2,1)}, u32[]{:S(2)}, u32[]{:S(2)}) async-start(bf16[32,64,512]{2,1,0:T(8,128)(2,1)} %gather_fusion.1), calls=%async_computation | async-start | bytes 4194304 | tf_op jit(solution)/shard_map/all_to_all | solution.py:165
  25.3 19.5 %collective-permute-start.1 = (bf16[8,64,512]{2,1,0:T(8,128)(2,1)S(1)}, bf16[8,64,512]{2,1,0:T(8,128)(2,1)}, u32[]{:S(2)}, u32[]{:S(2)}) collective-permute-start(bf16[8,64,512]{2,1,0:T(8,128)(2,1)S(1)} %get-tuple-element.35), channel_id=1, source_target_pairs={{0,1},{1,0},{2,3},{3,2},{4,5},{5,4},{6,7},{7,6},{8,9},{9,8},{10,11... | collective-permute-start | bytes 1572872 | tf_op jit(solution)/shard_map/ppermute | solution.py:163
  34.5 5.0 %copy-start.22 = (s32[16,4]{0,1:T(4,128)S(1)}, s32[16,4]{0,1:T(4,128)}, u32[]{:S(2)}) copy-start(s32[16,4]{0,1:T(4,128)} %param.10) | copy-start | bytes 772
  34.5 5.9 %copy-start.1 = (bf16[1024,512]{1,0:T(8,128)(2,1)S(1)}, bf16[1024,512]{1,0:T(8,128)(2,1)}, u32[]{:S(2)}) copy-start(bf16[1024,512]{1,0:T(8,128)(2,1)} %param.7) | copy-start | bytes 3145732
  39.7 3.4 %copy-start.23 = (bf16[512,512]{1,0:T(8,128)(2,1)S(1)}, bf16[512,512]{1,0:T(8,128)(2,1)}, u32[]{:S(2)}) copy-start(bf16[512,512]{1,0:T(8,128)(2,1)} %param.9) | copy-start | bytes 1572868
  68.6 1.7 copy-start.4
  68.7 14.9 %collective-permute-start.2 = (bf16[8,64,512]{2,1,0:T(8,128)(2,1)S(1)}, bf16[8,64,512]{2,1,0:T(8,128)(2,1)S(1)}, u32[]{:S(2)}, u32[]{:S(2)}) collective-permute-start(bf16[8,64,512]{2,1,0:T(8,128)(2,1)S(1)} %get-tuple-element.33), channel_id=1, source_target_pairs={{0,1},{1,0},{2,3},{3,2},{4,5},{5,4},{6,7},{7,6},{8,9},{9,8},{10,11... | collective-permute-start | bytes 1572872 | tf_op jit(solution)/shard_map/ppermute | solution.py:167
  70.3 1.4 copy-start.5
  71.7 66.2 %copy-start.12 = (bf16[2048,512]{1,0:T(8,128)(2,1)}, bf16[2048,512]{1,0:T(8,128)(2,1)S(1)}, u32[]{:S(2)}) copy-start(bf16[2048,512]{1,0:T(8,128)(2,1)S(1)} %pad_maximum_fusion) | copy-start | bytes 6291460
  83.6 53.5 %copy-start.17 = (bf16[8,2,64,512]{3,2,1,0:T(8,128)(2,1)}, bf16[8,2,64,512]{3,2,1,0:T(8,128)(2,1)S(1)}, u32[]{:S(2)}) copy-start(bf16[8,2,64,512]{3,2,1,0:T(8,128)(2,1)S(1)} %maximum_select_fusion.2) | copy-start | bytes 3145732
  124.2 3.1 %copy-start.11 = (bf16[8,1024,128]{2,1,0:T(8,128)(2,1)S(1)}, bf16[8,1024,128]{2,1,0:T(8,128)(2,1)}, u32[]{:S(2)}) copy-start(bf16[8,1024,128]{2,1,0:T(8,128)(2,1)} %get-tuple-element.16) | copy-start | bytes 6291460
  127.2 2.6 %copy-start.2 = (bf16[16,1024,128]{2,1,0:T(8,128)(2,1)S(1)}, bf16[16,1024,128]{2,1,0:T(8,128)(2,1)}, u32[]{:S(2)}) copy-start(bf16[16,1024,128]{2,1,0:T(8,128)(2,1)} %get-tuple-element.15) | copy-start | bytes 12582916
  131.1 3.5 %copy-start.15 = (f32[8,128,512]{2,1,0:T(8,128)}, f32[8,128,512]{2,1,0:T(8,128)S(1)}, u32[]{:S(2)}) copy-start(f32[8,128,512]{2,1,0:T(8,128)S(1)} %fusion.9) | copy-start | bytes 6291460
  131.1 2.0 copy-start.7
  131.1 3.0 %copy-start.19 = (bf16[8,128,512]{2,1,0:T(8,128)(2,1)S(1)}, bf16[8,128,512]{2,1,0:T(8,128)(2,1)}, u32[]{:S(2)}) copy-start(bf16[8,128,512]{2,1,0:T(8,128)(2,1)} %get-tuple-element.13) | copy-start | bytes 3145732
  135.6 14.0 %collective-permute-start.3 = (bf16[8,64,512]{2,1,0:T(8,128)(2,1)S(1)}, bf16[8,64,512]{2,1,0:T(8,128)(2,1)S(1)}, u32[]{:S(2)}, u32[]{:S(2)}) collective-permute-start(bf16[8,64,512]{2,1,0:T(8,128)(2,1)S(1)} %get-tuple-element.31), channel_id=1, source_target_pairs={{0,1},{1,0},{2,3},{3,2},{4,5},{5,4},{6,7},{7,6},{8,9},{9,8},{10,11... | collective-permute-start | bytes 1572872 | tf_op jit(solution)/shard_map/ppermute | solution.py:215
  151.7 11.9 %copy-start.16 = (bf16[8,2,1,256,128]{4,3,2,1,0:T(8,128)(2,1)S(1)}, bf16[8,2,1,256,128]{4,3,2,1,0:T(8,128)(2,1)}, u32[]{:S(2)}) copy-start(bf16[8,2,1,256,128]{4,3,2,1,0:T(8,128)(2,1)} %get-tuple-element.28) | copy-start | bytes 3145732
  151.7 51.3 %all-to-all-start.1 = ((bf16[32,64,512]{2,1,0:T(8,128)(2,1)}), bf16[32,64,512]{2,1,0:T(8,128)(2,1)}, u32[]{:S(2)}, u32[]{:S(2)}) async-start(bf16[32,64,512]{2,1,0:T(8,128)(2,1)} %gather_fusion.4), calls=%async_computation.1 | async-start | bytes 4194304 | tf_op jit(solution)/shard_map/all_to_all | solution.py:221
  162.0 3.6 %copy-start.20 = (bf16[8,128,512]{2,1,0:T(8,128)(2,1)S(1)}, bf16[8,128,512]{2,1,0:T(8,128)(2,1)}, u32[]{:S(2)}) copy-start(bf16[8,128,512]{2,1,0:T(8,128)(2,1)} %get-tuple-element.13) | copy-start | bytes 3145732
  162.0 25.7 %collective-permute-start.4 = (bf16[512,1024]{0,1:T(8,128)(2,1)}, bf16[512,1024]{0,1:T(8,128)(2,1)S(1)}, u32[]{:S(2)}, u32[]{:S(2)}) collective-permute-start(bf16[512,1024]{0,1:T(8,128)(2,1)} %pad_maximum_fusion.2), channel_id=1, source_target_pairs={{0,1},{1,0},{2,3},{3,2},{4,5},{5,4},{6,7},{7,6},{8,9},{9,8},{10,11... | collective-permute-start | bytes 3145736 | tf_op jit(solution)/shard_map/ppermute | solution.py:222
  163.6 2.5 %copy-start.8 = (bf16[8,128,512]{2,1,0:T(8,128)(2,1)S(1)}, bf16[8,128,512]{2,1,0:T(8,128)(2,1)}, u32[]{:S(2)}) copy-start(bf16[8,128,512]{2,1,0:T(8,128)(2,1)} %get-tuple-element.14) | copy-start | bytes 3145732
  165.6 1.6 copy-start.10
  165.6 2.2 copy-start.13
  189.3 4.4 %copy-start.18 = (bf16[8,64,512]{2,1,0:T(8,128)(2,1)S(1)}, bf16[8,64,512]{2,1,0:T(8,128)(2,1)}, u32[]{:S(2)}) copy-start(bf16[8,64,512]{2,1,0:T(8,128)(2,1)} %fusion.20) | copy-start | bytes 1572868
  193.6 2.0 collective-permute-start.5
  193.7 14.4 %collective-permute-start.6 = (bf16[8,64,512]{2,1,0:T(8,128)(2,1)S(1)}, bf16[8,64,512]{2,1,0:T(8,128)(2,1)}, u32[]{:S(2)}, u32[]{:S(2)}) collective-permute-start(bf16[8,64,512]{2,1,0:T(8,128)(2,1)S(1)} %copy-done.18), channel_id=1, source_target_pairs={{0,1},{1,0},{2,3},{3,2},{4,5},{5,4},{6,7},{7,6},{8,9},{9,8},{10,11... | collective-permute-start | bytes 1572872 | tf_op jit(solution)/shard_map/ppermute | solution.py:223
  205.2 6.3 %copy-start.6 = (bf16[512,1536]{1,0:T(8,128)(2,1)S(1)}, bf16[512,1536]{1,0:T(8,128)(2,1)}, u32[]{:S(2)}) copy-start(bf16[512,1536]{1,0:T(8,128)(2,1)} %reshape.222) | copy-start | bytes 4718596
  205.5 6.0 %copy-start.3 = (bf16[16,1024,128]{2,1,0:T(8,128)(2,1)S(1)}, bf16[16,1024,128]{2,1,0:T(8,128)(2,1)}, u32[]{:S(2)}) copy-start(bf16[16,1024,128]{2,1,0:T(8,128)(2,1)} %get-tuple-element.15) | copy-start | bytes 12582916
  209.9 12.9 %copy-start.24 = (bf16[512,512]{1,0:T(8,128)(2,1)S(1)}, bf16[512,512]{1,0:T(8,128)(2,1)}, u32[]{:S(2)}) copy-start(bf16[512,512]{1,0:T(8,128)(2,1)} %param.9) | copy-start | bytes 1572868
  209.9 15.8 %collective-permute-start.7 = (bf16[8,64,512]{2,1,0:T(8,128)(2,1)S(1)}, bf16[8,64,512]{2,1,0:T(8,128)(2,1)}, u32[]{:S(2)}, u32[]{:S(2)}) collective-permute-start(bf16[8,64,512]{2,1,0:T(8,128)(2,1)S(1)} %get-tuple-element.27), channel_id=1, source_target_pairs={{0,1},{1,0},{2,3},{3,2},{4,5},{5,4},{6,7},{7,6},{8,9},{9,8},{10,11... | collective-permute-start | bytes 1572872 | tf_op jit(solution)/shard_map/ppermute | solution.py:232
  214.1 23.5 %all-to-all-start.2 = ((bf16[8,32,1024]{2,1,0:T(8,128)(2,1)}), bf16[8,32,1024]{2,1,0:T(8,128)(2,1)}, u32[]{:S(2)}, u32[]{:S(2)}) async-start(bf16[8,32,1024]{2,1,0:T(8,128)(2,1)} %fusion.8), calls=%async_computation.2 | async-start | bytes 1048576 | tf_op jit(solution)/shard_map/all_to_all | solution.py:233
  226.9 1.2 copy-start.9
  226.9 1.9 copy-start.14

commit v3 on v2

--- a/solution.py
+++ b/solution.py
@@ -5,6 +5,7 @@
 from jax.experimental.pallas import tpu as pltpu
 from jax.sharding import PartitionSpec as P
 
+
 H = 8
 NBR = 4
 F32 = jnp.float32
@@ -17,7 +18,6 @@
     block_size, width = q_ref.shape[1], q_ref.shape[2]
     head_dim = width // H
     pair = 2 * head_dim
-    reach = (NBR + 1) * block_size
     scale = head_dim ** (-0.5)
 
     @pl.when(step == 0)
@@ -125,7 +125,7 @@
     )(scalars, query, cot, kv, kv_far, tiles)
 
 
-def body(node_feats, w_qkv, w_out, neighbours, tiles, partner, layer_cot):
+def layer(node_feats, w_qkv, w_out, neighbours, tiles, partner, layer_cot):
     rows, width = node_feats.shape
     parts = lax.axis_size("dom")
     groups = lax.axis_size("head")
@@ -190,50 +190,49 @@
     def back(x):
         return jnp.einsum("bcn,dc->bnd", x, w_kv, preferred_element_type=F32)
 
-    core = lax.axis_index("dom") % 2
-    chip_swap = [(i, i ^ 1) for i in range(parts)]
-    same_core = [[i for i in range(parts) if i % 2 == c] for c in range(2)]
+    place = lax.axis_index("dom")
 
     def rows_in(spec, a, b):
         return jnp.einsum(spec, a, b, preferred_element_type=F32)
 
     near_rows = feats_near.reshape(blocks, block_size, width)
     far_rows = feats_far.reshape(own, block_size, width)
-    near_split = dnear.reshape(blocks, 2, groups, span, block_size)
-    far_split = dfar.reshape(own, 2, groups, span, block_size)
-
-    def group_of(i):
-        cols = lambda x: lax.dynamic_slice_in_dim(x, i * span, span, 1)
-        dw_q = rows_in("rd,rc->dc", node_feats, cols(dq))
-        near = lax.dynamic_index_in_dim(near_split, i, 2, keepdims=False).reshape(blocks, 2 * span, block_size)
-        far = lax.dynamic_index_in_dim(far_split, i, 2, keepdims=False).reshape(own, 2 * span, block_size)
-        dw_kv = rows_in("bnd,bcn->dc", near_rows, near) + rows_in("bnd,bcn->dc", far_rows, far)
-        dw_out = rows_in("rc,rd->cd", layer_cot, cols(attended))
-        return dw_q, dw_kv, dw_out
 
     far_grad = back(dfar).astype(BF16).reshape(own, 2, half, width)
     far_peer = lax.ppermute(pick(far_grad, 1 - me), "head", swap)
-    dw_send = jnp.concatenate([x.astype(BF16) for x in group_of(1 - me)], axis=1)
+    dw_q = rows_in("rd,rc->dc", node_feats, dq)
+    dw_kv = rows_in("bnd,bcn->dc", near_rows, dnear) + rows_in("bnd,bcn->dc", far_rows, dfar)
+    dw_out = rows_in("rc,rd->cd", layer_cot, attended)
+    pieces = (dw_q, dw_kv[:, :width], dw_kv[:, width:], dw_out)
+    dw_all = jnp.stack(
+        [jnp.concatenate([x[:, g * span:(g + 1) * span] for x in pieces], axis=1) for g in range(groups)]
+    )
     peer_grad = back(dnear[own:]).reshape(own, 2, half, width)
-    early_send = pick(peer_grad, 1 - me).astype(BF16)
-    far_peer, dw_send, early_send = lax.optimization_barrier((far_peer, dw_send, early_send))
+    far_peer, dw_all = lax.optimization_barrier((far_peer, dw_all))
     half_grad = jnp.concatenate([pick(far_grad, me), far_peer], axis=0)
     returned = lax.all_to_all(half_grad[recv_from], "dom", split_axis=0, concat_axis=0, tiled=True)
-    dw_peer = lax.ppermute(dw_send, "head", swap)
-    early = lax.ppermute(early_send, "head", swap)
-
-    dw_mine = jnp.concatenate(group_of(me), axis=1) + dw_peer.astype(F32)
-    dw_mine = dw_mine.reshape(parts // 2, 2, width // parts, 4 * span)
-    dw_core = lax.ppermute(pick(dw_mine, 1 - core).astype(BF16), "dom", chip_swap)
-    dw_half = (pick(dw_mine, core) + dw_core.astype(F32)).astype(BF16)
-    returned, dw_half = lax.optimization_barrier((returned, dw_half))
+
+    def halve(x, axis, bit, name, pairs):
+        take = lambda i: lax.dynamic_index_in_dim(x, i, axis, keepdims=False)
+        got = lax.ppermute(take(1 - bit).astype(BF16), name, pairs)
+        return take(bit) + got.astype(F32)
+
+    def dom_stage(x, k, axis):
+        pairs = [(i, i ^ (1 << k)) for i in range(parts)]
+        shape = x.shape[:axis] + (x.shape[axis] // 2, 2) + x.shape[axis + 1:]
+        return halve(x.reshape(shape), axis + 1, (place >> k) & 1, "dom", pairs)
+
+    dw_sum = dom_stage(dw_all.reshape(groups, parts, width // parts, 4 * span), 0, 1)
+    dw_sum = halve(dw_sum, 0, me, "head", swap)
+    early = lax.ppermute(pick(peer_grad, 1 - me).astype(BF16), "head", swap)
+    dw_sum = dom_stage(dw_sum, 1, 0)
+    returned, dw_sum = lax.optimization_barrier((returned, dw_sum))
 
     returned = returned[send_slot].astype(F32)
     late = lax.ppermute((pick(peer_grad, me) + returned[own:]).astype(BF16), "head", swap)
-    dw_parts = lax.all_to_all(
-        dw_half, "dom", split_axis=0, concat_axis=0, tiled=True, axis_index_groups=same_core
-    )
-    dw_sum = jnp.sum(dw_parts.astype(F32), axis=0)
+    for k in range(2, parts.bit_length() - 1):
+        dw_sum = dom_stage(dw_sum, k, 0)
+    dw_sum = dw_sum[0]
 
     layer_out = project(attended, w_out)
     own_grad = (
@@ -256,7 +255,7 @@
         P(("dom", "head"), None),
     )
     return jax.shard_map(
-        body,
+        layer,
         mesh=mesh,
         in_specs=placed,
         out_specs=(

time: 241 us -> 236 us (0.979)
    ppermute x8 -> x11, starting transfers between devices: 12.6 us -> 22 us  [the longest x5 12.2 us: halve(): got = lax.ppermute(take(1 - bit).astype(BF16), name, pairs)]
    all_to_all x3 -> x2, starting transfers between devices: 25.1 us -> 16.4 us  [the longest x1 10.1 us: layer(): lax.all_to_all(half_grad[recv_from], 'dom', split_axis=0, concat_axis=0,...]
    all_to_all x3 -> x2, waiting for transfers between devices: 30.4 us -> 24.1 us  [the longest x1 24.1 us: layer(): lax.all_to_all(half_feats[send_from], 'dom', split_axis=0, concat_axis=0,...]
    optimization_barrier x0 -> x1, local copies, waits for them, and re-layouts: none -> 5.43 us  [layer(): far_peer, dw_all = lax.optimization_barrier((far_peer, dw_all))]
    ppermute x8 -> x11, waiting for transfers between devices: 48.6 us -> 53.3 us  [the longest x5 20.5 us: halve(): got = lax.ppermute(take(1 - bit).astype(BF16), name, pairs)]
    reshape x1, local copies, waits for them, and re-layouts: 4.97 us -> 1.92 us  [layer(): w_qkv.reshape(width, groups, 3, span).transpose(0, 2, 1, 3)]
    add x1 -> x0, local copies, waits for them, and re-layouts: 2.99 us -> none  [body(): dw_mine = jnp.concatenate(group_of(me), axis=1) + dw_peer.astype(F32)]
    dynamic_slice x2 -> x0, local copies, waits for them, and re-layouts: 2.97 us -> none  [the longest x1 1.82 us: group_of(): lax.dynamic_index_in_dim(near_split, i, 2, keepdims=False)]
  transfers between devices with their start and end apart: 11 -> 13, of which waited for: 9 -> 9; matrix products, arithmetic and copies ran while one was open for 22% -> 21% of each run, Pallas kernels for 0% -> 0%
where the time goes in v3:
time: 236 us; the launch traced here: 235 us
  waiting for transfers between devices  77.5 us (33%)
  starting transfers between devices  38.5 us (16%)
  Pallas kernels  37.8 us (16%)
  local copies, waits for them, and re-layouts  37.4 us (16%)
  matrix products  30.2 us (13%)
  other arithmetic  12.5 us (5%)
    pallas_call x1, Pallas kernels, attention(): pl.pallas_call(attention_kernel, grid_spec=grid_spec, out_shape=[jax.Shap...  37.8 us
    all_to_all x1, waiting for transfers between devices, layer(): lax.all_to_all(half_feats[send_from], 'dom', split_axis=0, concat_axis=0,...  24.1 us
    ppermute x5, waiting for transfers between devices, halve(): got = lax.ppermute(take(1 - bit).astype(BF16), name, pairs)  20.5 us
    dot_general x5, matrix products, project(): return jnp.dot(x, w, preferred_element_type=F32).astype(BF16)  13.4 us
    ppermute x5, starting transfers between devices, halve(): got = lax.ppermute(take(1 - bit).astype(BF16), name, pairs)  12.2 us
    ppermute x1, waiting for transfers between devices, layer(): peer_a = lax.ppermute(pick(feats, 1 - me), 'head', swap)  10.2 us
    all_to_all x1, starting transfers between devices, layer(): lax.all_to_all(half_grad[recv_from], 'dom', split_axis=0, concat_axis=0,...  10.1 us
    ppermute x1, waiting for transfers between devices, layer(): far_peer = lax.ppermute(pick(far_grad, 1 - me), 'head', swap)  9.53 us
  transfers between devices with their start and end apart: 13, of which 9 were waited for; matrix products, arithmetic and copies ran while one was open for 21% of the time, Pallas kernels for 0%

profile of v3, /device:TPU:0, one launch (start us, length us, event | category | flops | bytes accessed | tf_op | source)
XLA Modules:
  0.0 235.1 jit_solution(17348369081964168867)
XLA Ops:
  0.7 2.2 dynamic-slice_bitcast_fusion.3
  2.9 3.0 %collective-permute-start = (bf16[8,64,512]{2,1,0:T(8,128)(2,1)S(1)}, bf16[8,64,512]{2,1,0:T(8,128)(2,1)S(1)}, u32[]{:S(2)}, u32[]{:S(2)}) collective-permute-start(bf16[8,64,512]{2,1,0:T(8,128)(2,1)S(1)} %get-tuple-element.36), channel_id=1, source_target_pairs={{0,1},{1,0},{2,3},{3,2},{4,5},{5,4},{6,7},{7,6},{8,9},{9,8},{10,11... | collective-permute-start | bytes 1572872 | tf_op jit(solution)/shard_map/ppermute | solution.py:162
  7.5 10.2 %collective-permute-done = bf16[8,64,512]{2,1,0:T(8,128)(2,1)S(1)} collective-permute-done((bf16[8,64,512]{2,1,0:T(8,128)(2,1)S(1)}, bf16[8,64,512]{2,1,0:T(8,128)(2,1)S(1)}, u32[]{:S(2)}, u32[]{:S(2)}) %collective-permute-start) | collective-permute-done | bytes 524320 | tf_op jit(solution)/shard_map/ppermute | solution.py:162
  17.8 1.3 pad_maximum_fusion.2
  19.1 2.0 gather_fusion.1
  21.1 6.3 %all-to-all-start = ((bf16[32,64,512]{2,1,0:T(8,128)(2,1)}), bf16[32,64,512]{2,1,0:T(8,128)(2,1)}, u32[]{:S(2)}, u32[]{:S(2)}) async-start(bf16[32,64,512]{2,1,0:T(8,128)(2,1)} %gather_fusion.1), calls=%async_computation | async-start | bytes 4194304 | tf_op jit(solution)/shard_map/all_to_all | solution.py:165
  27.4 1.6 collective-permute-start.1
  29.0 1.6 copy.36
  30.6 3.9 %copy.37 = bf16[512,3,2,256]{3,2,1,0:T(2,128)(2,1)S(1)} copy(bf16[512,3,2,256]{0,3,1,2:T(8,128)(2,1)} %bitcast.139) | data formatting | bytes 3145728 | tf_op jit(solution)/shard_map/transpose | solution.py:171
  34.6 1.9 reshape.201
  37.4 3.0 %convolution_convert_fusion.5 = bf16[1024,512]{1,0:T(8,128)(2,1)} fusion(bf16[1024,512]{1,0:T(8,128)(2,1)} %param.7, bf16[512,1536]{1,0:T(8,128)(2,1)} %reshape.201), kind=kOutput, calls=%fused_computation.21 | convolution fusion | flops 537395200 | bytes 2621440 | tf_op jit(solution)/shard_map/dot_general | solution.py:175
  40.4 1.7 convolution_convert_fusion.4
  43.0 1.4 maximum_select_fusion.1
  44.3 24.1 %all-to-all-done = bf16[32,64,512]{2,1,0:T(8,128)(2,1)} async-done(((bf16[32,64,512]{2,1,0:T(8,128)(2,1)}), bf16[32,64,512]{2,1,0:T(8,128)(2,1)}, u32[]{:S(2)}, u32[]{:S(2)}) %all-to-all-start) | async-done | bytes 2097184 | tf_op jit(solution)/shard_map/all_to_all | solution.py:165
  68.5 2.2 gather_fusion.3
  70.8 1.6 collective-permute-start.2
  72.5 1.3 copy-done.2
  73.8 4.4 %convolution_convert_fusion = bf16[2048,1024]{1,0:T(8,128)(2,1)} fusion(bf16[512,1536]{1,0:T(8,128)(2,1)S(1)} %copy-done.2, bf16[1024,512]{1,0:T(8,128)(2,1)S(1)} %bitcast.141, bf16[1024,512]{1,0:T(8,128)(2,1)S(1)} %copy-done.1), kind=kOutput, calls=%fused_computation.7 | convolution fusion | flops 2153775104 | bytes 7340032 | tf_op jit(solution)/shard_map/dot_general | solution.py:175
  78.1 7.5 %collective-permute-done.2 = bf16[8,64,512]{2,1,0:T(8,128)(2,1)S(1)} collective-permute-done((bf16[8,64,512]{2,1,0:T(8,128)(2,1)S(1)}, bf16[8,64,512]{2,1,0:T(8,128)(2,1)S(1)}, u32[]{:S(2)}, u32[]{:S(2)}) %collective-permute-start.2) | collective-permute-done | bytes 524320 | tf_op jit(solution)/shard_map/ppermute | solution.py:167
  85.7 2.6 %convolution_convert_fusion.1 = bf16[1024,1024]{1,0:T(8,128)(2,1)} fusion(bf16[1024,512]{1,0:T(8,128)(2,1)S(1)} %bitcast.151, bf16[512,1536]{1,0:T(8,128)(2,1)S(1)} %copy-done.2), kind=kOutput, calls=%fused_computation.17 | convolution fusion | flops 1074790400 | bytes 4194304 | tf_op jit(solution)/shard_map/dot_general | solution.py:175
  88.4 37.8 %attention.1 = (bf16[8,128,512]{2,1,0:T(8,128)(2,1)}, bf16[8,128,512]{2,1,0:T(8,128)(2,1)}, bf16[16,1024,128]{2,1,0:T(8,128)(2,1)}, bf16[8,1024,128]{2,1,0:T(8,128)(2,1)}) custom-call(s32[33]{0:T(128)} %pad_add_fusion.near_ref, bf16[8,128,512]{2,1,0:T(8,128)(2,1)} %bitcast.162, bf16[8,128,512]{2,1,0:T(8,128)(2,1)} %bitcast.163, ...), custom_call_target="tpu_custom_call" | custom-call | flops 32212254720 | bytes 10485760 | tf_op jit(solution)/shard_map/attention/pallas_call | solution.py:109
  126.2 3.0 %convolution_convert_fusion.2 = bf16[8,128,512]{2,1,0:T(8,128)(2,1)S(1)} fusion(bf16[8,1024,128]{2,1,0:T(8,128)(2,1)} %get-tuple-element.15, bf16[512,1536]{1,0:T(8,128)(2,1)S(1)} %copy-done.2), kind=kOutput, calls=%fused_computation.18 | convolution fusion | flops 1074266112 | bytes 4194304 | tf_op jit(solution)/shard_map/bcn,dc->bnd/dot_general | solution.py:191
  129.3 2.3 fusion.32
  136.9 1.6 collective-permute-start.3
  138.9 2.5 %pad_maximum_fusion = f32[2,512,1024]{1,2,0:T(8,128)} fusion(f32[1,512,1024]{1,2,0:T(8,128)S(1)} %maximum_bitcast_fusion.1, f32[1,512,1024]{1,2,0:T(8,128)S(1)} %maximum_bitcast_fusion), kind=kLoop, calls=%fused_computation.6 | loop fusion | flops 1048576 | bytes 8388608 | tf_op jit(solution)/shard_map/stack | solution.py:207
  141.4 9.5 %collective-permute-done.3 = bf16[8,64,512]{2,1,0:T(8,128)(2,1)S(1)} collective-permute-done((bf16[8,64,512]{2,1,0:T(8,128)(2,1)S(1)}, bf16[8,64,512]{2,1,0:T(8,128)(2,1)S(1)}, u32[]{:S(2)}, u32[]{:S(2)}) %collective-permute-start.3) | collective-permute-done | bytes 524320 | tf_op jit(solution)/shard_map/ppermute | solution.py:202
  151.0 2.0 gather_fusion.4
  153.0 10.1 %all-to-all-start.1 = ((bf16[32,64,512]{2,1,0:T(8,128)(2,1)}), bf16[32,64,512]{2,1,0:T(8,128)(2,1)}, u32[]{:S(2)}, u32[]{:S(2)}) async-start(bf16[32,64,512]{2,1,0:T(8,128)(2,1)} %gather_fusion.4), calls=%async_computation.1 | async-start | bytes 4194304 | tf_op jit(solution)/shard_map/all_to_all | solution.py:213
  163.2 5.4 %copy.46 = f32[2,512,1024]{2,1,0:T(8,128)} copy(f32[2,512,1024]{1,2,0:T(8,128)} %pad_maximum_fusion) | data formatting | bytes 8388608 | tf_op jit(solution)/shard_map/optimization_barrier | solution.py:211
  168.6 1.7 fusion.1
  170.8 2.5 %collective-permute-done.4 = bf16[2,8,32,1024]{3,2,1,0:T(8,128)(2,1)} collective-permute-done((bf16[2,8,32,1024]{3,2,1,0:T(8,128)(2,1)S(1)}, bf16[2,8,32,1024]{3,2,1,0:T(8,128)(2,1)}, u32[]{:S(2)}, u32[]{:S(2)}) %collective-permute-start.4) | collective-permute-done | bytes 1048608 | tf_op jit(solution)/shard_map/ppermute | solution.py:217
  173.2 2.2 bitcast_add_fusion.1
  176.3 1.5 collective-permute-start.5
  177.8 3.3 %fusion.4 = f32[8,128,512]{2,1,0:T(8,128)S(1)} fusion(bf16[16,1024,128]{2,1,0:T(8,128)(2,1)} %get-tuple-element.14, bf16[512,1536]{1,0:T(8,128)(2,1)} %reshape.201), kind=kOutput, calls=%fused_computation.35 | convolution fusion | flops 1073741824 | bytes 7340032 | tf_op jit(solution)/shard_map/bcn,dc->bnd/dot_general | solution.py:191
  182.5 8.9 %collective-permute-done.5 = bf16[8,32,1024]{2,1,0:T(8,128)(2,1)} collective-permute-done((bf16[8,32,1024]{2,1,0:T(8,128)(2,1)}, bf16[8,32,1024]{2,1,0:T(8,128)(2,1)}, u32[]{:S(2)}, u32[]{:S(2)}) %collective-permute-start.5) | collective-permute-done | bytes 524320 | tf_op jit(solution)/shard_map/ppermute | solution.py:217
  192.7 1.9 collective-permute-start.6
  194.6 2.6 %fusion.7 = f32[8,128,512]{2,1,0:T(8,128)} fusion(bf16[16,1024,128]{2,1,0:T(8,128)(2,1)S(1)} %copy-done.20, bf16[512,1536]{1,0:T(8,128)(2,1)S(1)} %copy-done.3), kind=kOutput, calls=%fused_computation.38 | convolution fusion | flops 1073741824 | bytes 7340032 | tf_op jit(solution)/shard_map/bcn,dc->bnd/dot_general | solution.py:191
  197.2 8.2 %collective-permute-done.6 = bf16[4,32,1024]{2,1,0:T(8,128)(2,1)S(1)} collective-permute-done((bf16[4,32,1024]{2,1,0:T(8,128)(2,1)S(1)}, bf16[4,32,1024]{2,1,0:T(8,128)(2,1)S(1)}, u32[]{:S(2)}, u32[]{:S(2)}) %collective-permute-start.6) | collective-permute-done | bytes 262176 | tf_op jit(solution)/shard_map/ppermute | solution.py:217
  205.5 5.5 %collective-permute-start.9 = (bf16[2,32,1024]{2,1,0:T(8,128)(2,1)S(1)}, bf16[2,32,1024]{2,1,0:T(8,128)(2,1)S(1)}, u32[]{:S(2)}, u32[]{:S(2)}) collective-permute-start(bf16[2,32,1024]{2,1,0:T(8,128)(2,1)S(1)} %fusion.20), channel_id=1, source_target_pairs={{0,8},{2,10},{4,12},{6,14},{8,0},{10,2},{12,4},{14,6},{16,24},{18,... | collective-permute-start | bytes 393224 | tf_op jit(solution)/shard_map/ppermute | solution.py:217
  211.0 2.2 gather_fusion.5
  213.5 1.3 copy-done.9
  214.8 1.4 fusion.3
  216.3 1.6 collective-permute-start.8
  217.9 2.9 %collective-permute-start.10 = (bf16[1,32,1024]{2,1,0:T(8,128)(2,1)S(1)}, bf16[1,32,1024]{2,1,0:T(8,128)(2,1)S(1)}, u32[]{:S(2)}, u32[]{:S(2)}) collective-permute-start(bf16[1,32,1024]{2,1,0:T(8,128)(2,1)S(1)} %dynamic-slice_convert_fusion.3), channel_id=1, source_target_pairs={{0,16},{2,18},{4,20},{6,22},{8,24},{10,26},{12,28},{14,30},{16,0},... | collective-permute-start | bytes 196616 | tf_op jit(solution)/shard_map/ppermute | solution.py:217
  220.8 1.7 convolution_convert_fusion.3
  224.7 5.6 %collective-permute-done.8 = bf16[8,64,512]{2,1,0:T(8,128)(2,1)S(1)} collective-permute-done((bf16[8,64,512]{2,1,0:T(8,128)(2,1)S(1)}, bf16[8,64,512]{2,1,0:T(8,128)(2,1)S(1)}, u32[]{:S(2)}, u32[]{:S(2)}) %collective-permute-start.8) | collective-permute-done | bytes 524320 | tf_op jit(solution)/shard_map/ppermute | solution.py:232
  230.7 1.3 copy-done.4
  232.3 2.8 %fusion = bf16[8,128,512]{2,1,0:T(8,128)(2,1)} fusion(f32[8,2,64,512]{3,2,1,0:T(8,128)S(1)} %maximum_select_fusion, f32[8,128,512]{2,1,0:T(8,128)S(1)} %copy-done.4, bf16[8,128,512]{2,1,0:T(8,128)(2,1)S(1)} %copy-done.11, bf16[512,1536]{1,0:T(8,128)(2,1)} %reshape.201), kind=kOutput, calls=%fused_computation.13 | convolution fusion | flops 538443776 | bytes 6815744 | tf_op jit(solution)/shard_map/rc,dc->rd/dot_general | solution.py:239
  (95 shorter events, 16.7 us)
Async XLA Ops:
  0.6 39.8 %copy-start = (bf16[1024,512]{1,0:T(8,128)(2,1)S(1)}, bf16[1024,512]{1,0:T(8,128)(2,1)}, u32[]{:S(2)}) copy-start(bf16[1024,512]{1,0:T(8,128)(2,1)} %param.13) | copy-start | bytes 3145732
  0.6 5.2 %copy-start.13 = (s32[16]{0:T(128)S(1)}, s32[16]{0:T(128)}, u32[]{:S(2)}) copy-start(s32[16]{0:T(128)} %param.12) | copy-start | bytes 196
  2.9 14.9 %collective-permute-start = (bf16[8,64,512]{2,1,0:T(8,128)(2,1)S(1)}, bf16[8,64,512]{2,1,0:T(8,128)(2,1)S(1)}, u32[]{:S(2)}, u32[]{:S(2)}) collective-permute-start(bf16[8,64,512]{2,1,0:T(8,128)(2,1)S(1)} %get-tuple-element.36), channel_id=1, source_target_pairs={{0,1},{1,0},{2,3},{3,2},{4,5},{5,4},{6,7},{7,6},{8,9},{9,8},{10,11... | collective-permute-start | bytes 1572872 | tf_op jit(solution)/shard_map/ppermute | solution.py:162
  17.8 3.3 %copy-start.5 = (bf16[8,64,512]{2,1,0:T(8,128)(2,1)}, bf16[8,64,512]{2,1,0:T(8,128)(2,1)S(1)}, u32[]{:S(2)}) copy-start(bf16[8,64,512]{2,1,0:T(8,128)(2,1)S(1)} %collective-permute-done) | copy-start | bytes 1572868
  21.1 7.9 %copy-start.7 = (bf16[512,1536]{1,0:T(8,128)(2,1)S(1)}, bf16[512,1536]{1,0:T(8,128)(2,1)}, u32[]{:S(2)}) copy-start(bf16[512,1536]{1,0:T(8,128)(2,1)} %param.8) | copy-start | bytes 4718596
  21.1 47.4 %all-to-all-start = ((bf16[32,64,512]{2,1,0:T(8,128)(2,1)}), bf16[32,64,512]{2,1,0:T(8,128)(2,1)}, u32[]{:S(2)}, u32[]{:S(2)}) async-start(bf16[32,64,512]{2,1,0:T(8,128)(2,1)} %gather_fusion.1), calls=%async_computation | async-start | bytes 4194304 | tf_op jit(solution)/shard_map/all_to_all | solution.py:165
  27.4 14.7 %collective-permute-start.1 = (bf16[8,64,512]{2,1,0:T(8,128)(2,1)}, bf16[8,64,512]{2,1,0:T(8,128)(2,1)S(1)}, u32[]{:S(2)}, u32[]{:S(2)}) collective-permute-start(bf16[8,64,512]{2,1,0:T(8,128)(2,1)} %get-tuple-element.37), channel_id=1, source_target_pairs={{0,1},{1,0},{2,3},{3,2},{4,5},{5,4},{6,7},{7,6},{8,9},{9,8},{10,11... | collective-permute-start | bytes 1572872 | tf_op jit(solution)/shard_map/ppermute | solution.py:163
  34.6 1.9 copy-start.14
  36.5 3.9 %copy-start.15 = (bf16[512,512]{1,0:T(8,128)(2,1)S(1)}, bf16[512,512]{1,0:T(8,128)(2,1)}, u32[]{:S(2)}) copy-start(bf16[512,512]{1,0:T(8,128)(2,1)} %param.9) | copy-start | bytes 1572868
  40.4 2.5 %copy-start.6 = (bf16[8,64,512]{2,1,0:T(8,128)(2,1)S(1)}, bf16[8,64,512]{2,1,0:T(8,128)(2,1)}, u32[]{:S(2)}) copy-start(bf16[8,64,512]{2,1,0:T(8,128)(2,1)} %copy-done.5) | copy-start | bytes 1572868
  42.1 0.8 copy-start.12
  70.7 1.7 copy-start.1
  70.8 14.9 %collective-permute-start.2 = (bf16[8,64,512]{2,1,0:T(8,128)(2,1)S(1)}, bf16[8,64,512]{2,1,0:T(8,128)(2,1)S(1)}, u32[]{:S(2)}, u32[]{:S(2)}) collective-permute-start(bf16[8,64,512]{2,1,0:T(8,128)(2,1)S(1)} %get-tuple-element.35), channel_id=1, source_target_pairs={{0,1},{1,0},{2,3},{3,2},{4,5},{5,4},{6,7},{7,6},{8,9},{9,8},{10,11... | collective-permute-start | bytes 1572872 | tf_op jit(solution)/shard_map/ppermute | solution.py:167
  72.4 1.4 copy-start.2
  126.2 3.1 %copy-start.19 = (bf16[16,1024,128]{2,1,0:T(8,128)(2,1)S(1)}, bf16[16,1024,128]{2,1,0:T(8,128)(2,1)}, u32[]{:S(2)}) copy-start(bf16[16,1024,128]{2,1,0:T(8,128)(2,1)} %get-tuple-element.14) | copy-start | bytes 12582916
  129.3 2.3 copy-start.21
  132.8 1.2 copy-start.10
  134.8 1.2 copy-start.17
  136.9 14.0 %collective-permute-start.3 = (bf16[8,64,512]{2,1,0:T(8,128)(2,1)S(1)}, bf16[8,64,512]{2,1,0:T(8,128)(2,1)S(1)}, u32[]{:S(2)}, u32[]{:S(2)}) collective-permute-start(bf16[8,64,512]{2,1,0:T(8,128)(2,1)S(1)} %get-tuple-element.29), channel_id=1, source_target_pairs={{0,1},{1,0},{2,3},{3,2},{4,5},{5,4},{6,7},{7,6},{8,9},{9,8},{10,11... | collective-permute-start | bytes 1572872 | tf_op jit(solution)/shard_map/ppermute | solution.py:202
  153.0 52.4 %all-to-all-start.1 = ((bf16[32,64,512]{2,1,0:T(8,128)(2,1)}), bf16[32,64,512]{2,1,0:T(8,128)(2,1)}, u32[]{:S(2)}, u32[]{:S(2)}) async-start(bf16[32,64,512]{2,1,0:T(8,128)(2,1)} %gather_fusion.4), calls=%async_computation.1 | async-start | bytes 4194304 | tf_op jit(solution)/shard_map/all_to_all | solution.py:213
  170.4 2.9 %collective-permute-start.4 = (bf16[2,8,32,1024]{3,2,1,0:T(8,128)(2,1)S(1)}, bf16[2,8,32,1024]{3,2,1,0:T(8,128)(2,1)}, u32[]{:S(2)}, u32[]{:S(2)}) collective-permute-start(bf16[2,8,32,1024]{3,2,1,0:T(8,128)(2,1)S(1)} %fusion.1), channel_id=1, source_target_pairs={{0,2},{2,0},{4,6},{6,4},{8,10},{10,8},{12,14},{14,12},{16,18},{18,... | collective-permute-start | bytes 3145736 | tf_op jit(solution)/shard_map/ppermute | solution.py:217
  176.3 15.1 %collective-permute-start.5 = (bf16[8,32,1024]{2,1,0:T(8,128)(2,1)}, bf16[8,32,1024]{2,1,0:T(8,128)(2,1)}, u32[]{:S(2)}, u32[]{:S(2)}) collective-permute-start(bf16[8,32,1024]{2,1,0:T(8,128)(2,1)} %fusion.14), channel_id=1, source_target_pairs={{0,1},{1,0},{2,3},{3,2},{4,5},{5,4},{6,7},{7,6},{8,9},{9,8},{10,11... | collective-permute-start | bytes 1572872 | tf_op jit(solution)/shard_map/ppermute | solution.py:217
  177.8 16.7 %copy-start.20 = (bf16[16,1024,128]{2,1,0:T(8,128)(2,1)S(1)}, bf16[16,1024,128]{2,1,0:T(8,128)(2,1)}, u32[]{:S(2)}) copy-start(bf16[16,1024,128]{2,1,0:T(8,128)(2,1)} %get-tuple-element.14) | copy-start | bytes 12582916
  181.1 11.5 %copy-start.8 = (f32[8,128,512]{2,1,0:T(8,128)}, f32[8,128,512]{2,1,0:T(8,128)S(1)}, u32[]{:S(2)}) copy-start(f32[8,128,512]{2,1,0:T(8,128)S(1)} %fusion.4) | copy-start | bytes 6291460
  181.1 13.4 %copy-start.3 = (bf16[512,1536]{1,0:T(8,128)(2,1)S(1)}, bf16[512,1536]{1,0:T(8,128)(2,1)}, u32[]{:S(2)}) copy-start(bf16[512,1536]{1,0:T(8,128)(2,1)} %reshape.201) | copy-start | bytes 4718596
  182.0 31.5 %collective-permute-start.7 = (bf16[8,64,512]{2,1,0:T(8,128)(2,1)}, bf16[8,64,512]{2,1,0:T(8,128)(2,1)}, u32[]{:S(2)}, u32[]{:S(2)}) collective-permute-start(bf16[8,64,512]{2,1,0:T(8,128)(2,1)} %fusion.15), channel_id=1, source_target_pairs={{0,1},{1,0},{2,3},{3,2},{4,5},{5,4},{6,7},{7,6},{8,9},{9,8},{10,11... | collective-permute-start | bytes 1572872 | tf_op jit(solution)/shard_map/ppermute | solution.py:227
  192.7 12.7 %collective-permute-start.6 = (bf16[4,32,1024]{2,1,0:T(8,128)(2,1)S(1)}, bf16[4,32,1024]{2,1,0:T(8,128)(2,1)S(1)}, u32[]{:S(2)}, u32[]{:S(2)}) collective-permute-start(bf16[4,32,1024]{2,1,0:T(8,128)(2,1)S(1)} %fusion.19), channel_id=1, source_target_pairs={{0,4},{2,6},{4,0},{6,2},{8,12},{10,14},{12,8},{14,10},{16,20},{18,... | collective-permute-start | bytes 786440 | tf_op jit(solution)/shard_map/ppermute | solution.py:217
  205.5 12.3 %collective-permute-start.9 = (bf16[2,32,1024]{2,1,0:T(8,128)(2,1)S(1)}, bf16[2,32,1024]{2,1,0:T(8,128)(2,1)S(1)}, u32[]{:S(2)}, u32[]{:S(2)}) collective-permute-start(bf16[2,32,1024]{2,1,0:T(8,128)(2,1)S(1)} %fusion.20), channel_id=1, source_target_pairs={{0,8},{2,10},{4,12},{6,14},{8,0},{10,2},{12,4},{14,6},{16,24},{18,... | collective-permute-start | bytes 393224 | tf_op jit(solution)/shard_map/ppermute | solution.py:217
  213.2 1.6 copy-start.9
  213.5 7.3 %copy-start.16 = (bf16[512,512]{1,0:T(8,128)(2,1)S(1)}, bf16[512,512]{1,0:T(8,128)(2,1)}, u32[]{:S(2)}) copy-start(bf16[512,512]{1,0:T(8,128)(2,1)} %param.9) | copy-start | bytes 1572868
  213.5 7.2 %copy-start.18 = (bf16[8,128,512]{2,1,0:T(8,128)(2,1)S(1)}, bf16[8,128,512]{2,1,0:T(8,128)(2,1)}, u32[]{:S(2)}) copy-start(bf16[8,128,512]{2,1,0:T(8,128)(2,1)} %get-tuple-element.12) | copy-start | bytes 3145732
  216.3 14.0 %collective-permute-start.8 = (bf16[8,64,512]{2,1,0:T(8,128)(2,1)S(1)}, bf16[8,64,512]{2,1,0:T(8,128)(2,1)S(1)}, u32[]{:S(2)}, u32[]{:S(2)}) collective-permute-start(bf16[8,64,512]{2,1,0:T(8,128)(2,1)S(1)} %get-tuple-element.23), channel_id=1, source_target_pairs={{0,1},{1,0},{2,3},{3,2},{4,5},{5,4},{6,7},{7,6},{8,9},{9,8},{10,11... | collective-permute-start | bytes 1572872 | tf_op jit(solution)/shard_map/ppermute | solution.py:232
  217.9 5.5 %collective-permute-start.10 = (bf16[1,32,1024]{2,1,0:T(8,128)(2,1)S(1)}, bf16[1,32,1024]{2,1,0:T(8,128)(2,1)S(1)}, u32[]{:S(2)}, u32[]{:S(2)}) collective-permute-start(bf16[1,32,1024]{2,1,0:T(8,128)(2,1)S(1)} %dynamic-slice_convert_fusion.3), channel_id=1, source_target_pairs={{0,16},{2,18},{4,20},{6,22},{8,24},{10,26},{12,28},{14,30},{16,0},... | collective-permute-start | bytes 196616 | tf_op jit(solution)/shard_map/ppermute | solution.py:217
  230.4 1.6 copy-start.4
  230.4 1.9 copy-start.11

commit v4 on v3

--- a/solution.py
+++ b/solution.py
@@ -159,13 +159,22 @@
     recv_from = jnp.sum(jnp.where(recv_slot[None, :] == all_slots[:, None], iota[None, :], 0), axis=1)
 
     feats = node_feats.reshape(own, 2, half, width)
-    peer_a = lax.ppermute(pick(feats, 1 - me), "head", swap)
-    peer_b = lax.ppermute(pick(feats, me), "head", swap)
-    half_feats = jnp.concatenate([pick(feats, me), peer_a], axis=0)
-    incoming = lax.all_to_all(half_feats[send_from], "dom", split_axis=0, concat_axis=0, tiled=True)
-    half_far = incoming[recv_slot]
-    other_far = lax.ppermute(half_far[own:], "head", swap)
-    feats_far = halves(half_far[:own], other_far)
+    split = [slice(c * width // 2, (c + 1) * width // 2) for c in range(2)]
+    mine, give = pick(feats, me), pick(feats, 1 - me)
+
+    def over_dom(x, source):
+        return lax.all_to_all(x[source], "dom", split_axis=0, concat_axis=0, tiled=True)
+
+    a_pieces = [lax.ppermute(give[:, :, c], "head", swap) for c in split]
+    far_mine, far_other = [], []
+    for c, got in zip(split, a_pieces):
+        piece = over_dom(jnp.concatenate([mine[:, :, c], got], axis=0), send_from)[recv_slot]
+        far_mine.append(piece[:own])
+        far_other.append(lax.ppermute(piece[own:], "head", swap))
+    later, _ = lax.optimization_barrier((mine, a_pieces[1]))
+    peer_b = lax.ppermute(later, "head", swap)
+    peer_a = jnp.concatenate(a_pieces, axis=2)
+    feats_far = halves(jnp.concatenate(far_mine, axis=2), jnp.concatenate(far_other, axis=2))
     feats_peer = halves(peer_a, peer_b)
 
     w_split = w_qkv.reshape(width, groups, 3, span).transpose(0, 2, 1, 3).reshape(width, 3 * width)
@@ -199,7 +208,9 @@
     far_rows = feats_far.reshape(own, block_size, width)
 
     far_grad = back(dfar).astype(BF16).reshape(own, 2, half, width)
-    far_peer = lax.ppermute(pick(far_grad, 1 - me), "head", swap)
+    far_own, far_give = pick(far_grad, me), pick(far_grad, 1 - me)
+    far_peer0 = lax.ppermute(far_give[:, :, split[0]], "head", swap)
+    far_peer = lax.ppermute(far_give[:, :, split[1]], "head", swap)
     dw_q = rows_in("rd,rc->dc", node_feats, dq)
     dw_kv = rows_in("bnd,bcn->dc", near_rows, dnear) + rows_in("bnd,bcn->dc", far_rows, dfar)
     dw_out = rows_in("rc,rd->cd", layer_cot, attended)
@@ -209,8 +220,8 @@
     )
     peer_grad = back(dnear[own:]).reshape(own, 2, half, width)
     far_peer, dw_all = lax.optimization_barrier((far_peer, dw_all))
-    half_grad = jnp.concatenate([pick(far_grad, me), far_peer], axis=0)
-    returned = lax.all_to_all(half_grad[recv_from], "dom", split_axis=0, concat_axis=0, tiled=True)
+    returned0 = over_dom(jnp.concatenate([far_own[:, :, split[0]], far_peer0], axis=0), recv_from)
+    returned = over_dom(jnp.concatenate([far_own[:, :, split[1]], far_peer], axis=0), recv_from)
 
     def halve(x, axis, bit, name, pairs):
         take = lambda i: lax.dynamic_index_in_dim(x, i, axis, keepdims=False)
@@ -226,10 +237,20 @@
     dw_sum = halve(dw_sum, 0, me, "head", swap)
     early = lax.ppermute(pick(peer_grad, 1 - me).astype(BF16), "head", swap)
     dw_sum = dom_stage(dw_sum, 1, 0)
-    returned, dw_sum = lax.optimization_barrier((returned, dw_sum))
-
-    returned = returned[send_slot].astype(F32)
-    late = lax.ppermute((pick(peer_grad, me) + returned[own:]).astype(BF16), "head", swap)
+    late_near = pick(peer_grad, me)
+    late_second = late_near[:, :, split[1]]
+    returned, dw_sum, late_second = lax.optimization_barrier((returned, dw_sum, late_second))
+
+    late_pieces = (late_near[:, :, split[0]], late_second)
+    back_pieces = [x[send_slot].astype(F32) for x in (returned0, returned)]
+    late = jnp.concatenate(
+        [
+            lax.ppermute((near + x[own:]).astype(BF16), "head", swap)
+            for near, x in zip(late_pieces, back_pieces)
+        ],
+        axis=2,
+    )
+    returned = jnp.concatenate([x[:own] for x in back_pieces], axis=2)
     for k in range(2, parts.bit_length() - 1):
         dw_sum = dom_stage(dw_sum, k, 0)
     dw_sum = dw_sum[0]
@@ -239,7 +260,7 @@
         jnp.einsum("rc,dc->rd", dq, w_query, preferred_element_type=F32).reshape(own, block_size, width)
         + back(dnear[:own])
     )
-    feat_grad = own_grad + halves(returned[:own] + early.astype(F32), late.astype(F32))
+    feat_grad = own_grad + halves(returned + early.astype(F32), late.astype(F32))
     feat_grad = feat_grad.astype(BF16).reshape(rows, width)
     return (layer_out, feat_grad, dw_sum[:, : 3 * span], dw_sum[:, 3 * span:].T)
 

time: 236 us -> 236 us (level)
  waiting for transfers between devices: 77.5 us -> 54.8 us
  local copies, waits for them, and re-layouts: 37.4 us -> 48.6 us
  starting transfers between devices: 38.5 us -> 46.2 us
    ppermute x5 -> x9, waiting for transfers between devices: 32.8 us -> 21.4 us  [the longest x1 9.24 us: layer(): peer_b = lax.ppermute(later, 'head', swap)]
    all_to_all x2 -> x4, waiting for transfers between devices: 24.1 us -> 13.3 us  [over_dom(): lax.all_to_all(x[source], 'dom', split_axis=0, concat_axis=0, tiled=True)]
    all_to_all x2 -> x4, starting transfers between devices: 16.4 us -> 25.8 us  [over_dom(): lax.all_to_all(x[source], 'dom', split_axis=0, concat_axis=0, tiled=True)]
    gather x4 -> x8, local copies, waits for them, and re-layouts: 8.39 us -> 15.3 us  [the longest x4 6.43 us: over_dom(): x[source]]
    ppermute x5, starting transfers between devices: 12.2 us -> 5.93 us  [halve(): got = lax.ppermute(take(1 - bit).astype(BF16), name, pairs)]
    slice x0 -> x8, local copies, waits for them, and re-layouts: none -> 5.2 us  [the longest x2 2.85 us: layer(): far_mine.append(piece[:own])]
    ppermute x5 -> x9, starting transfers between devices: 9.34 us -> 13.2 us  [the longest x2 4.58 us: layer(): a_pieces = [lax.ppermute(give[:, :, c], 'head', swap) for c in split]]
    unnamed x45 -> x49, local copies, waits for them, and re-layouts: 8.73 us -> 5.1 us
  transfers between devices with their start and end apart: 13 -> 19, of which waited for: 9 -> 11; matrix products, arithmetic and copies ran while one was open for 21% -> 33% of each run, Pallas kernels for 0% -> 0%
where the time goes in v4:
time: 236 us; the launch traced here: 234 us
  waiting for transfers between devices  54.8 us (23%)
  local copies, waits for them, and re-layouts  48.6 us (21%)
  starting transfers between devices  46.2 us (20%)
  Pallas kernels  37.9 us (16%)
  matrix products  31.7 us (13%)
  other arithmetic  14 us (6%)
    pallas_call x1, Pallas kernels, attention(): pl.pallas_call(attention_kernel, grid_spec=grid_spec, out_shape=[jax.Shap...  37.9 us
    all_to_all x4, starting transfers between devices, over_dom(): lax.all_to_all(x[source], 'dom', split_axis=0, concat_axis=0, tiled=True)  25.8 us
    ppermute x5, waiting for transfers between devices, halve(): got = lax.ppermute(take(1 - bit).astype(BF16), name, pairs)  20.2 us
    all_to_all x4, waiting for transfers between devices, over_dom(): lax.all_to_all(x[source], 'dom', split_axis=0, concat_axis=0, tiled=True)  13.3 us
    dot_general x5, matrix products, project(): return jnp.dot(x, w, preferred_element_type=F32).astype(BF16)  13.1 us
    dot_general x3, matrix products, back(): return jnp.einsum('bcn,dc->bnd', x, w_kv, preferred_element_type=F32)  9.74 us
    ppermute x1, waiting for transfers between devices, layer(): peer_b = lax.ppermute(later, 'head', swap)  9.24 us
    ppermute x2, waiting for transfers between devices, layer(): far_other.append(lax.ppermute(piece[own:], 'head', swap))  7.54 us
  transfers between devices with their start and end apart: 19, of which 11 were waited for; matrix products, arithmetic and copies ran while one was open for 33% of the time, Pallas kernels for 0%

profile of v4, /device:TPU:0, one launch (start us, length us, event | category | flops | bytes accessed | tf_op | source)
XLA Modules:
  0.0 234.4 jit_solution(10646886438616725803)
XLA Ops:
  2.8 3.0 %collective-permute-start.1 = (bf16[8,64,256]{2,1,0:T(8,128)(2,1)S(1)}, bf16[8,64,256]{2,1,0:T(8,128)(2,1)S(1)}, u32[]{:S(2)}, u32[]{:S(2)}) collective-permute-start(bf16[8,64,256]{2,1,0:T(8,128)(2,1)S(1)} %get-tuple-element.51), channel_id=1, source_target_pairs={{0,1},{1,0},{2,3},{3,2},{4,5},{5,4},{6,7},{7,6},{8,9},{9,8},{10,11... | collective-permute-start | bytes 786440 | tf_op jit(solution)/shard_map/ppermute | solution.py:168
  8.2 3.8 %collective-permute-done.1 = bf16[8,64,256]{2,1,0:T(8,128)(2,1)S(1)} collective-permute-done((bf16[8,64,256]{2,1,0:T(8,128)(2,1)S(1)}, bf16[8,64,256]{2,1,0:T(8,128)(2,1)S(1)}, u32[]{:S(2)}, u32[]{:S(2)}) %collective-permute-start.1) | collective-permute-done | bytes 262176 | tf_op jit(solution)/shard_map/ppermute | solution.py:168
  12.1 1.6 gather_fusion.4
  13.7 6.3 %all-to-all-start.1 = ((bf16[32,64,256]{2,1,0:T(8,128)(2,1)}), bf16[32,64,256]{2,1,0:T(8,128)(2,1)}, u32[]{:S(2)}, u32[]{:S(2)}) async-start(bf16[32,64,256]{2,1,0:T(8,128)(2,1)} %gather_fusion.4), calls=%async_computation.1 | async-start | bytes 2097152 | tf_op jit(solution)/shard_map/all_to_all | solution.py:166
  20.1 1.6 collective-permute-start
  21.6 1.6 copy.38
  23.2 3.9 %copy.39 = bf16[512,3,2,256]{3,2,1,0:T(2,128)(2,1)S(1)} copy(bf16[512,3,2,256]{0,3,1,2:T(8,128)(2,1)} %bitcast.142) | data formatting | bytes 3145728 | tf_op jit(solution)/shard_map/transpose | solution.py:180
  27.2 1.9 reshape.230
  30.5 1.6 gather_fusion.1
  32.1 10.9 %all-to-all-done.1 = bf16[32,64,256]{2,1,0:T(8,128)(2,1)} async-done(((bf16[32,64,256]{2,1,0:T(8,128)(2,1)}), bf16[32,64,256]{2,1,0:T(8,128)(2,1)}, u32[]{:S(2)}, u32[]{:S(2)}) %all-to-all-start.1) | async-done | bytes 1048608 | tf_op jit(solution)/shard_map/all_to_all | solution.py:166
  43.0 6.8 %all-to-all-start = ((bf16[32,64,256]{2,1,0:T(8,128)(2,1)}), bf16[32,64,256]{2,1,0:T(8,128)(2,1)}, u32[]{:S(2)}, u32[]{:S(2)}) async-start(bf16[32,64,256]{2,1,0:T(8,128)(2,1)} %gather_fusion.1), calls=%async_computation | async-start | bytes 2097152 | tf_op jit(solution)/shard_map/all_to_all | solution.py:166
  49.9 2.7 %convolution_convert_fusion.5 = bf16[1024,512]{1,0:T(8,128)(2,1)} fusion(bf16[1024,512]{1,0:T(8,128)(2,1)S(1)} %copy-done.1, bf16[512,1536]{1,0:T(8,128)(2,1)} %reshape.230), kind=kOutput, calls=%fused_computation.25 | convolution fusion | flops 537395200 | bytes 2621440 | tf_op jit(solution)/shard_map/dot_general | solution.py:184
  52.6 1.5 collective-permute-start.2
  54.7 1.7 convolution_convert_fusion.4
  57.5 9.2 %collective-permute-done.2 = bf16[8,64,512]{2,1,0:T(8,128)(2,1)S(1)} collective-permute-done((bf16[8,64,512]{2,1,0:T(8,128)(2,1)S(1)}, bf16[8,64,512]{2,1,0:T(8,128)(2,1)S(1)}, u32[]{:S(2)}, u32[]{:S(2)}) %collective-permute-start.2) | collective-permute-done | bytes 524320 | tf_op jit(solution)/shard_map/ppermute | solution.py:175
  66.9 4.4 %convolution_convert_fusion = bf16[2048,1024]{1,0:T(8,128)(2,1)} fusion(bf16[512,1536]{1,0:T(8,128)(2,1)S(1)} %copy-done.2, bf16[1024,512]{1,0:T(8,128)(2,1)S(1)} %bitcast.143, bf16[1024,512]{1,0:T(8,128)(2,1)S(1)} %copy-done.1), kind=kOutput, calls=%fused_computation.11 | convolution fusion | flops 2153775104 | bytes 7340032 | tf_op jit(solution)/shard_map/dot_general | solution.py:184
  71.2 2.6 %gather_fusion.5 = bf16[16,64,256]{2,1,0:T(8,128)(2,1)} fusion(bf16[32,64,256]{2,1,0:T(8,128)(2,1)} %all-to-all-done.1, s32[1024]{0:T(1024)S(1)} %pad_clamp_fusion.2), kind=kCustom, calls=%fused_computation.5 | custom fusion | bytes 1048640 | tf_op jit(solution)/shard_map/gather | solution.py:171
  73.9 1.8 fusion.36
  75.7 1.5 collective-permute-start.4
  77.2 2.6 %gather_fusion.3 = bf16[16,64,256]{2,1,0:T(8,128)(2,1)} fusion(bf16[32,64,256]{2,1,0:T(8,128)(2,1)} %all-to-all-done, s32[1024]{0:T(1024)S(1)} %pad_clamp_fusion.2), kind=kCustom, calls=%fused_computation.3 | custom fusion | bytes 1048640 | tf_op jit(solution)/shard_map/gather | solution.py:171
  81.7 2.8 %collective-permute-done.4 = bf16[8,64,256]{2,1,0:T(8,128)(2,1)} collective-permute-done((bf16[8,64,256]{2,1,0:T(8,128)(2,1)}, bf16[8,64,256]{2,1,0:T(8,128)(2,1)}, u32[]{:S(2)}, u32[]{:S(2)}) %collective-permute-start.4) | collective-permute-done | bytes 262176 | tf_op jit(solution)/shard_map/ppermute | solution.py:173
  84.5 4.7 %collective-permute-done.3 = bf16[8,64,256]{2,1,0:T(8,128)(2,1)S(1)} collective-permute-done((bf16[8,64,256]{2,1,0:T(8,128)(2,1)S(1)}, bf16[8,64,256]{2,1,0:T(8,128)(2,1)S(1)}, u32[]{:S(2)}, u32[]{:S(2)}) %collective-permute-start.3) | collective-permute-done | bytes 262176 | tf_op jit(solution)/shard_map/ppermute | solution.py:173
  90.3 2.7 %convolution_convert_fusion.1 = bf16[1024,1024]{1,0:T(8,128)(2,1)} fusion(bf16[1024,512]{1,0:T(8,128)(2,1)S(1)} %bitcast.153, bf16[512,1536]{1,0:T(8,128)(2,1)S(1)} %copy-done.3), kind=kOutput, calls=%fused_computation.21 | convolution fusion | flops 1074790400 | bytes 4194304 | tf_op jit(solution)/shard_map/dot_general | solution.py:184
  93.0 37.9 %attention.1 = (bf16[8,128,512]{2,1,0:T(8,128)(2,1)}, bf16[8,128,512]{2,1,0:T(8,128)(2,1)}, bf16[16,1024,128]{2,1,0:T(8,128)(2,1)}, bf16[8,1024,128]{2,1,0:T(8,128)(2,1)}) custom-call(s32[33]{0:T(128)} %pad_add_fusion.near_ref, bf16[8,128,512]{2,1,0:T(8,128)(2,1)} %bitcast.165, bf16[8,128,512]{2,1,0:T(8,128)(2,1)} %bitcast.166, ...), custom_call_target="tpu_custom_call" | custom-call | flops 32212254720 | bytes 10485760 | tf_op jit(solution)/shard_map/attention/pallas_call | solution.py:109
  130.9 2.9 %convolution_convert_fusion.2 = bf16[8,128,512]{2,1,0:T(8,128)(2,1)S(1)} fusion(bf16[8,1024,128]{2,1,0:T(8,128)(2,1)} %get-tuple-element.18, bf16[512,1536]{1,0:T(8,128)(2,1)S(1)} %copy-done.3), kind=kOutput, calls=%fused_computation.22 | convolution fusion | flops 1074266112 | bytes 4194304 | tf_op jit(solution)/shard_map/bcn,dc->bnd/dot_general | solution.py:200
  136.2 2.3 fusion.39
  142.8 1.7 convolution_bitcast_fusion
  146.0 1.6 gather_fusion.6
  147.6 5.8 %all-to-all-start.2 = ((bf16[32,64,256]{2,1,0:T(8,128)(2,1)}), bf16[32,64,256]{2,1,0:T(8,128)(2,1)}, u32[]{:S(2)}, u32[]{:S(2)}) async-start(bf16[32,64,256]{2,1,0:T(8,128)(2,1)} %gather_fusion.6), calls=%async_computation.2 | async-start | bytes 2097152 | tf_op jit(solution)/shard_map/all_to_all | solution.py:166
  155.9 2.5 %pad_maximum_fusion = f32[2,512,1024]{1,2,0:T(8,128)} fusion(f32[1,512,1024]{1,2,0:T(8,128)S(1)} %maximum_bitcast_fusion.1, f32[1,512,1024]{1,2,0:T(8,128)S(1)} %maximum_bitcast_fusion), kind=kLoop, calls=%fused_computation.10 | loop fusion | flops 1048576 | bytes 8388608 | tf_op jit(solution)/shard_map/stack | solution.py:218
  158.4 5.4 %copy.48 = f32[2,512,1024]{2,1,0:T(8,128)} copy(f32[2,512,1024]{1,2,0:T(8,128)} %pad_maximum_fusion) | data formatting | bytes 8388608 | tf_op jit(solution)/shard_map/optimization_barrier | solution.py:222
  163.9 2.8 %fusion.1 = bf16[2,8,32,1024]{3,2,1,0:T(8,128)(2,1)} fusion(f32[2,8,2,32,1024]{4,3,2,1,0:T(8,128)} %bitcast.140, s32[]{:T(128)S(6)} %select_n.187), kind=kLoop, calls=%fused_computation.28 | loop fusion | bytes 2097156 | tf_op jit(solution)/shard_map/convert_element_type | solution.py:228
  167.1 4.2 %fusion.3 = f32[8,128,512]{2,1,0:T(8,128)} fusion(bf16[16,1024,128]{2,1,0:T(8,128)(2,1)} %get-tuple-element.17, bf16[512,1536]{1,0:T(8,128)(2,1)S(1)} %copy-done.4), kind=kOutput, calls=%fused_computation.35 | convolution fusion | flops 1073741824 | bytes 7340032 | tf_op jit(solution)/shard_map/bcn,dc->bnd/dot_general | solution.py:200
  172.3 1.7 gather_fusion.8
  173.9 2.4 %all-to-all-done.2 = bf16[32,64,256]{2,1,0:T(8,128)(2,1)} async-done(((bf16[32,64,256]{2,1,0:T(8,128)(2,1)}), bf16[32,64,256]{2,1,0:T(8,128)(2,1)}, u32[]{:S(2)}, u32[]{:S(2)}) %all-to-all-start.2) | async-done | bytes 1048608 | tf_op jit(solution)/shard_map/all_to_all | solution.py:166
  176.3 6.9 %all-to-all-start.3 = ((bf16[32,64,256]{2,1,0:T(8,128)(2,1)}), bf16[32,64,256]{2,1,0:T(8,128)(2,1)}, u32[]{:S(2)}, u32[]{:S(2)}) async-start(bf16[32,64,256]{2,1,0:T(8,128)(2,1)} %gather_fusion.8), calls=%async_computation.3 | async-start | bytes 2097152 | tf_op jit(solution)/shard_map/all_to_all | solution.py:166
  183.2 2.4 %bitcast_add_fusion.1 = f32[2,8,32,1024]{3,2,1,0:T(8,128)S(1)} fusion(bf16[2,8,32,1024]{3,2,1,0:T(8,128)(2,1)} %collective-permute-done.7, f32[2,8,2,32,1024]{4,3,2,1,0:T(8,128)} %bitcast.141, s32[]{:T(128)S(6)} %select_n.186), kind=kLoop, calls=%fused_computation.18 | loop fusion | flops 1048576 | bytes 5242884 | tf_op jit(solution)/shard_map/add | solution.py:229
  188.7 2.6 %fusion.6 = f32[8,128,512]{2,1,0:T(8,128)} fusion(bf16[16,1024,128]{2,1,0:T(8,128)(2,1)S(1)} %copy-done.22, bf16[512,1536]{1,0:T(8,128)(2,1)S(1)} %copy-done.5), kind=kOutput, calls=%fused_computation.38 | convolution fusion | flops 1073741824 | bytes 7340032 | tf_op jit(solution)/shard_map/bcn,dc->bnd/dot_general | solution.py:200
  191.4 9.2 %collective-permute-done.8 = bf16[8,32,1024]{2,1,0:T(8,128)(2,1)S(1)} collective-permute-done((bf16[8,32,1024]{2,1,0:T(8,128)(2,1)S(1)}, bf16[8,32,1024]{2,1,0:T(8,128)(2,1)S(1)}, u32[]{:S(2)}, u32[]{:S(2)}) %collective-permute-start.8) | collective-permute-done | bytes 524320 | tf_op jit(solution)/shard_map/ppermute | solution.py:228
  200.7 1.9 collective-permute-start.9
  202.7 1.7 convolution_convert_fusion.3
  204.3 6.3 %collective-permute-done.9 = bf16[4,32,1024]{2,1,0:T(8,128)(2,1)S(1)} collective-permute-done((bf16[4,32,1024]{2,1,0:T(8,128)(2,1)S(1)}, bf16[4,32,1024]{2,1,0:T(8,128)(2,1)S(1)}, u32[]{:S(2)}, u32[]{:S(2)}) %collective-permute-start.9) | collective-permute-done | bytes 262176 | tf_op jit(solution)/shard_map/ppermute | solution.py:228
  211.6 1.8 gather_fusion.7
  213.6 1.8 gather_fusion.9
  219.8 1.9 collective-permute-done.13
  221.7 1.9 collective-permute-start.14
  224.8 2.8 %collective-permute-done.14 = bf16[1,32,1024]{2,1,0:T(8,128)(2,1)S(1)} collective-permute-done((bf16[1,32,1024]{2,1,0:T(8,128)(2,1)S(1)}, bf16[1,32,1024]{2,1,0:T(8,128)(2,1)S(1)}, u32[]{:S(2)}, u32[]{:S(2)}) %collective-permute-start.14) | collective-permute-done | bytes 65568 | tf_op jit(solution)/shard_map/ppermute | solution.py:228
  231.6 2.8 %fusion = bf16[8,128,512]{2,1,0:T(8,128)(2,1)} fusion(f32[8,2,64,512]{3,2,1,0:T(8,128)S(1)} %maximum_select_fusion, f32[8,128,512]{2,1,0:T(8,128)S(1)} %copy-done.6, bf16[8,128,512]{2,1,0:T(8,128)(2,1)S(1)} %copy-done.14, bf16[512,1536]{1,0:T(8,128)(2,1)} %reshape.230), kind=kOutput, calls=%fused_computation.17 | convolution fusion | flops 538443776 | bytes 6815744 | tf_op jit(solution)/shard_map/rc,dc->rd/dot_general | solution.py:260
  (131 shorter events, 36.6 us)
Async XLA Ops:
  0.6 54.1 %copy-start = (bf16[1024,512]{1,0:T(8,128)(2,1)S(1)}, bf16[1024,512]{1,0:T(8,128)(2,1)}, u32[]{:S(2)}) copy-start(bf16[1024,512]{1,0:T(8,128)(2,1)} %param.13) | copy-start | bytes 3145732
  0.6 5.2 %copy-start.15 = (s32[16]{0:T(128)S(1)}, s32[16]{0:T(128)}, u32[]{:S(2)}) copy-start(s32[16]{0:T(128)} %param.12) | copy-start | bytes 196
  2.8 9.3 %collective-permute-start.1 = (bf16[8,64,256]{2,1,0:T(8,128)(2,1)S(1)}, bf16[8,64,256]{2,1,0:T(8,128)(2,1)S(1)}, u32[]{:S(2)}, u32[]{:S(2)}) collective-permute-start(bf16[8,64,256]{2,1,0:T(8,128)(2,1)S(1)} %get-tuple-element.51), channel_id=1, source_target_pairs={{0,1},{1,0},{2,3},{3,2},{4,5},{5,4},{6,7},{7,6},{8,9},{9,8},{10,11... | collective-permute-start | bytes 786440 | tf_op jit(solution)/shard_map/ppermute | solution.py:168
  13.7 7.9 %copy-start.11 = (bf16[512,1536]{1,0:T(8,128)(2,1)S(1)}, bf16[512,1536]{1,0:T(8,128)(2,1)}, u32[]{:S(2)}) copy-start(bf16[512,1536]{1,0:T(8,128)(2,1)} %param.8) | copy-start | bytes 4718596
  13.7 29.3 %all-to-all-start.1 = ((bf16[32,64,256]{2,1,0:T(8,128)(2,1)}), bf16[32,64,256]{2,1,0:T(8,128)(2,1)}, u32[]{:S(2)}, u32[]{:S(2)}) async-start(bf16[32,64,256]{2,1,0:T(8,128)(2,1)} %gather_fusion.4), calls=%async_computation.1 | async-start | bytes 2097152 | tf_op jit(solution)/shard_map/all_to_all | solution.py:166
  20.1 9.3 %collective-permute-start = (bf16[8,64,256]{2,1,0:T(8,128)(2,1)}, bf16[8,64,256]{2,1,0:T(8,128)(2,1)}, u32[]{:S(2)}, u32[]{:S(2)}) collective-permute-start(bf16[8,64,256]{2,1,0:T(8,128)(2,1)} %get-tuple-element.50), channel_id=1, source_target_pairs={{0,1},{1,0},{2,3},{3,2},{4,5},{5,4},{6,7},{7,6},{8,9},{9,8},{10,11... | collective-permute-start | bytes 786440 | tf_op jit(solution)/shard_map/ppermute | solution.py:168
  27.2 1.9 copy-start.16
  30.5 19.4 %copy-start.1 = (bf16[1024,512]{1,0:T(8,128)(2,1)S(1)}, bf16[1024,512]{1,0:T(8,128)(2,1)}, u32[]{:S(2)}) copy-start(bf16[1024,512]{1,0:T(8,128)(2,1)} %param.7) | copy-start | bytes 3145732
  32.1 22.6 %copy-start.17 = (bf16[512,512]{1,0:T(8,128)(2,1)S(1)}, bf16[512,512]{1,0:T(8,128)(2,1)}, u32[]{:S(2)}) copy-start(bf16[512,512]{1,0:T(8,128)(2,1)} %param.9) | copy-start | bytes 1572868
  43.0 34.2 %all-to-all-start = ((bf16[32,64,256]{2,1,0:T(8,128)(2,1)}), bf16[32,64,256]{2,1,0:T(8,128)(2,1)}, u32[]{:S(2)}, u32[]{:S(2)}) async-start(bf16[32,64,256]{2,1,0:T(8,128)(2,1)} %gather_fusion.1), calls=%async_computation | async-start | bytes 2097152 | tf_op jit(solution)/shard_map/all_to_all | solution.py:166
  52.6 14.2 %collective-permute-start.2 = (bf16[8,64,512]{2,1,0:T(8,128)(2,1)S(1)}, bf16[8,64,512]{2,1,0:T(8,128)(2,1)S(1)}, u32[]{:S(2)}, u32[]{:S(2)}) collective-permute-start(bf16[8,64,512]{2,1,0:T(8,128)(2,1)S(1)} %get-tuple-element.14), channel_id=1, source_target_pairs={{0,1},{1,0},{2,3},{3,2},{4,5},{5,4},{6,7},{7,6},{8,9},{9,8},{10,11... | collective-permute-start | bytes 1572872 | tf_op jit(solution)/shard_map/ppermute | solution.py:175
  56.4 10.5 %copy-start.2 = (bf16[512,1536]{1,0:T(8,128)(2,1)S(1)}, bf16[512,1536]{1,0:T(8,128)(2,1)}, u32[]{:S(2)}) copy-start(bf16[512,1536]{1,0:T(8,128)(2,1)} %reshape.230) | copy-start | bytes 4718596
  75.7 8.8 %collective-permute-start.4 = (bf16[8,64,256]{2,1,0:T(8,128)(2,1)}, bf16[8,64,256]{2,1,0:T(8,128)(2,1)}, u32[]{:S(2)}, u32[]{:S(2)}) collective-permute-start(bf16[8,64,256]{2,1,0:T(8,128)(2,1)} %get-tuple-element.47), channel_id=1, source_target_pairs={{0,1},{1,0},{2,3},{3,2},{4,5},{5,4},{6,7},{7,6},{8,9},{9,8},{10,11... | collective-permute-start | bytes 786440 | tf_op jit(solution)/shard_map/ppermute | solution.py:173
  80.9 8.3 %collective-permute-start.3 = (bf16[8,64,256]{2,1,0:T(8,128)(2,1)S(1)}, bf16[8,64,256]{2,1,0:T(8,128)(2,1)S(1)}, u32[]{:S(2)}, u32[]{:S(2)}) collective-permute-start(bf16[8,64,256]{2,1,0:T(8,128)(2,1)S(1)} %get-tuple-element.45), channel_id=1, source_target_pairs={{0,1},{1,0},{2,3},{3,2},{4,5},{5,4},{6,7},{7,6},{8,9},{9,8},{10,11... | collective-permute-start | bytes 786440 | tf_op jit(solution)/shard_map/ppermute | solution.py:173
  81.6 8.7 %copy-start.3 = (bf16[512,1536]{1,0:T(8,128)(2,1)S(1)}, bf16[512,1536]{1,0:T(8,128)(2,1)}, u32[]{:S(2)}) copy-start(bf16[512,1536]{1,0:T(8,128)(2,1)} %reshape.230) | copy-start | bytes 4718596
  133.8 2.4 %copy-start.21 = (bf16[16,1024,128]{2,1,0:T(8,128)(2,1)S(1)}, bf16[16,1024,128]{2,1,0:T(8,128)(2,1)}, u32[]{:S(2)}) copy-start(bf16[16,1024,128]{2,1,0:T(8,128)(2,1)} %get-tuple-element.17) | copy-start | bytes 12582916
  134.6 11.3 %collective-permute-start.5 = (bf16[8,64,256]{2,1,0:T(8,128)(2,1)S(1)}, bf16[8,64,256]{2,1,0:T(8,128)(2,1)S(1)}, u32[]{:S(2)}, u32[]{:S(2)}) collective-permute-start(bf16[8,64,256]{2,1,0:T(8,128)(2,1)S(1)} %get-tuple-element.42), channel_id=1, source_target_pairs={{0,1},{1,0},{2,3},{3,2},{4,5},{5,4},{6,7},{7,6},{8,9},{9,8},{10,11... | collective-permute-start | bytes 786440 | tf_op jit(solution)/shard_map/ppermute | solution.py:212
  136.2 2.3 copy-start.23
  139.8 1.8 copy-start.13
  141.6 1.2 copy-start.19
  144.5 13.9 %collective-permute-start.6 = (bf16[8,64,256]{2,1,0:T(8,128)(2,1)}, bf16[8,64,256]{2,1,0:T(8,128)(2,1)}, u32[]{:S(2)}, u32[]{:S(2)}) collective-permute-start(bf16[8,64,256]{2,1,0:T(8,128)(2,1)} %get-tuple-element.43), channel_id=1, source_target_pairs={{0,1},{1,0},{2,3},{3,2},{4,5},{5,4},{6,7},{7,6},{8,9},{9,8},{10,11... | collective-permute-start | bytes 786440 | tf_op jit(solution)/shard_map/ppermute | solution.py:213
  147.6 7.1 %copy-start.8 = (f32[512,256]{0,1:T(8,128)S(1)}, f32[512,256]{0,1:T(8,128)}, u32[]{:S(2)}) copy-start(f32[512,256]{0,1:T(8,128)} %get-tuple-element.26) | copy-start | bytes 1572868
  147.6 28.7 %all-to-all-start.2 = ((bf16[32,64,256]{2,1,0:T(8,128)(2,1)}), bf16[32,64,256]{2,1,0:T(8,128)(2,1)}, u32[]{:S(2)}, u32[]{:S(2)}) async-start(bf16[32,64,256]{2,1,0:T(8,128)(2,1)} %gather_fusion.6), calls=%async_computation.2 | async-start | bytes 2097152 | tf_op jit(solution)/shard_map/all_to_all | solution.py:166
  153.4 1.4 copy-start.9
  154.7 1.0 copy-start.7
  163.9 3.2 %copy-start.4 = (bf16[512,1536]{1,0:T(8,128)(2,1)S(1)}, bf16[512,1536]{1,0:T(8,128)(2,1)}, u32[]{:S(2)}) copy-start(bf16[512,1536]{1,0:T(8,128)(2,1)} %reshape.230) | copy-start | bytes 4718596
  166.7 16.5 %collective-permute-start.7 = (bf16[2,8,32,1024]{3,2,1,0:T(8,128)(2,1)}, bf16[2,8,32,1024]{3,2,1,0:T(8,128)(2,1)}, u32[]{:S(2)}, u32[]{:S(2)}) collective-permute-start(bf16[2,8,32,1024]{3,2,1,0:T(8,128)(2,1)} %fusion.1), channel_id=1, source_target_pairs={{0,2},{2,0},{4,6},{6,4},{8,10},{10,8},{12,14},{14,12},{16,18},{18,... | collective-permute-start | bytes 3145736 | tf_op jit(solution)/shard_map/ppermute | solution.py:228
  176.3 37.3 %all-to-all-start.3 = ((bf16[32,64,256]{2,1,0:T(8,128)(2,1)}), bf16[32,64,256]{2,1,0:T(8,128)(2,1)}, u32[]{:S(2)}, u32[]{:S(2)}) async-start(bf16[32,64,256]{2,1,0:T(8,128)(2,1)} %gather_fusion.8), calls=%async_computation.3 | async-start | bytes 2097152 | tf_op jit(solution)/shard_map/all_to_all | solution.py:166
  183.2 3.2 %copy-start.12 = (f32[8,128,512]{2,1,0:T(8,128)S(1)}, f32[8,128,512]{2,1,0:T(8,128)}, u32[]{:S(2)}) copy-start(f32[8,128,512]{2,1,0:T(8,128)} %fusion.3) | copy-start | bytes 6291460
  183.2 5.5 %copy-start.22 = (bf16[16,1024,128]{2,1,0:T(8,128)(2,1)S(1)}, bf16[16,1024,128]{2,1,0:T(8,128)(2,1)}, u32[]{:S(2)}) copy-start(bf16[16,1024,128]{2,1,0:T(8,128)(2,1)} %get-tuple-element.17) | copy-start | bytes 12582916
  185.6 3.1 %copy-start.5 = (bf16[512,1536]{1,0:T(8,128)(2,1)S(1)}, bf16[512,1536]{1,0:T(8,128)(2,1)}, u32[]{:S(2)}) copy-start(bf16[512,1536]{1,0:T(8,128)(2,1)} %reshape.230) | copy-start | bytes 4718596
  185.7 14.9 %collective-permute-start.8 = (bf16[8,32,1024]{2,1,0:T(8,128)(2,1)S(1)}, bf16[8,32,1024]{2,1,0:T(8,128)(2,1)S(1)}, u32[]{:S(2)}, u32[]{:S(2)}) collective-permute-start(bf16[8,32,1024]{2,1,0:T(8,128)(2,1)S(1)} %fusion.13), channel_id=1, source_target_pairs={{0,1},{1,0},{2,3},{3,2},{4,5},{5,4},{6,7},{7,6},{8,9},{9,8},{10,11... | collective-permute-start | bytes 1572872 | tf_op jit(solution)/shard_map/ppermute | solution.py:228
  187.3 36.4 %collective-permute-start.10 = (bf16[8,64,512]{2,1,0:T(8,128)(2,1)}, bf16[8,64,512]{2,1,0:T(8,128)(2,1)}, u32[]{:S(2)}, u32[]{:S(2)}) collective-permute-start(bf16[8,64,512]{2,1,0:T(8,128)(2,1)} %fusion.14), channel_id=1, source_target_pairs={{0,1},{1,0},{2,3},{3,2},{4,5},{5,4},{6,7},{7,6},{8,9},{9,8},{10,11... | collective-permute-start | bytes 1572872 | tf_op jit(solution)/shard_map/ppermute | solution.py:238
  191.4 11.3 %copy-start.18 = (bf16[512,512]{1,0:T(8,128)(2,1)S(1)}, bf16[512,512]{1,0:T(8,128)(2,1)}, u32[]{:S(2)}) copy-start(bf16[512,512]{1,0:T(8,128)(2,1)} %param.9) | copy-start | bytes 1572868
  191.4 11.3 %copy-start.20 = (bf16[8,128,512]{2,1,0:T(8,128)(2,1)S(1)}, bf16[8,128,512]{2,1,0:T(8,128)(2,1)}, u32[]{:S(2)}) copy-start(bf16[8,128,512]{2,1,0:T(8,128)(2,1)} %get-tuple-element.15) | copy-start | bytes 3145732
  200.7 9.9 %collective-permute-start.9 = (bf16[4,32,1024]{2,1,0:T(8,128)(2,1)S(1)}, bf16[4,32,1024]{2,1,0:T(8,128)(2,1)S(1)}, u32[]{:S(2)}, u32[]{:S(2)}) collective-permute-start(bf16[4,32,1024]{2,1,0:T(8,128)(2,1)S(1)} %fusion.20), channel_id=1, source_target_pairs={{0,4},{2,6},{4,0},{6,2},{8,12},{10,14},{12,8},{14,10},{16,20},{18,... | collective-permute-start | bytes 786440 | tf_op jit(solution)/shard_map/ppermute | solution.py:228
  215.5 6.2 %copy-start.10 = (f32[4,32,1024]{2,1,0:T(8,128)S(1)}, f32[4,32,1024]{2,1,0:T(8,128)}, u32[]{:S(2)}) copy-start(f32[4,32,1024]{2,1,0:T(8,128)} %bitcast_add_fusion.4) | copy-start | bytes 1572868
  216.6 5.0 %collective-permute-start.13 = (bf16[2,32,1024]{2,1,0:T(8,128)(2,1)S(1)}, bf16[2,32,1024]{2,1,0:T(8,128)(2,1)S(1)}, u32[]{:S(2)}, u32[]{:S(2)}) collective-permute-start(bf16[2,32,1024]{2,1,0:T(8,128)(2,1)S(1)} %fusion.21), channel_id=1, source_target_pairs={{0,8},{2,10},{4,12},{6,14},{8,0},{10,2},{12,4},{14,6},{16,24},{18,... | collective-permute-start | bytes 393224 | tf_op jit(solution)/shard_map/ppermute | solution.py:228
  217.7 11.2 %collective-permute-start.12 = (bf16[8,64,256]{2,1,0:T(8,128)(2,1)S(1)}, bf16[8,64,256]{2,1,0:T(8,128)(2,1)S(1)}, u32[]{:S(2)}, u32[]{:S(2)}) collective-permute-start(bf16[8,64,256]{2,1,0:T(8,128)(2,1)S(1)} %fusion.15), channel_id=1, source_target_pairs={{0,1},{1,0},{2,3},{3,2},{4,5},{5,4},{6,7},{7,6},{8,9},{9,8},{10,11... | collective-permute-start | bytes 786440 | tf_op jit(solution)/shard_map/ppermute | solution.py:248
  218.4 11.2 %collective-permute-start.11 = (bf16[8,64,256]{2,1,0:T(8,128)(2,1)S(1)}, bf16[8,64,256]{2,1,0:T(8,128)(2,1)S(1)}, u32[]{:S(2)}, u32[]{:S(2)}) collective-permute-start(bf16[8,64,256]{2,1,0:T(8,128)(2,1)S(1)} %get-tuple-element.30), channel_id=1, source_target_pairs={{0,1},{1,0},{2,3},{3,2},{4,5},{5,4},{6,7},{7,6},{8,9},{9,8},{10,11... | collective-permute-start | bytes 786440 | tf_op jit(solution)/shard_map/ppermute | solution.py:248
  221.7 5.9 %collective-permute-start.14 = (bf16[1,32,1024]{2,1,0:T(8,128)(2,1)S(1)}, bf16[1,32,1024]{2,1,0:T(8,128)(2,1)S(1)}, u32[]{:S(2)}, u32[]{:S(2)}) collective-permute-start(bf16[1,32,1024]{2,1,0:T(8,128)(2,1)S(1)} %dynamic-slice_convert_fusion.3), channel_id=1, source_target_pairs={{0,16},{2,18},{4,20},{6,22},{8,24},{10,26},{12,28},{14,30},{16,0},... | collective-permute-start | bytes 196616 | tf_op jit(solution)/shard_map/ppermute | solution.py:228
  229.8 1.6 copy-start.6
  229.8 1.9 copy-start.14
